TPU v7x, 256 devices: a whole 4x4x8 slice. The times are simulated.
256 devices in a mesh: leaf: 8 (over y, core), sub: 32 (over x, z).
Axes of the slice: x: 4, y: 4, z: 8, core: 2. Of those that a mesh axis runs over, the one named last changes fastest.
Arguments:
- points: bfloat16 [1048576, 32], P(('leaf', 'sub')), may hold values from -6 to 6
- vectors: bfloat16 [1048576, 2, 128], P(('leaf', 'sub')), may hold values from -6 to 6
- inv_length: float32 [32], replicated, may hold values from 0.15 to 0.5
- order: int32 [256, 4096], P(('leaf', 'sub')), may hold values from 0 to 4095, each once within a row
- leaf_basis: bfloat16 [2048, 512, 128], P(('leaf', 'sub')), may hold values from -0.25 to 0.25
- leaf_transfer: bfloat16 [2048, 128, 128], P(('leaf', 'sub')), may hold values from -0.5 to 0.5
- level_transfer: bfloat16 [8, 62, 128, 128], P('leaf'), may hold values from -0.5 to 0.5
- near_list: int32 [2048, 3], P(('leaf', 'sub')), may hold values from 0 to 2047, as said below
- near_count: int32 [2048], P(('leaf', 'sub')), may hold values from 1 to 3, as said below
- pair_list: int32 [256, 3], P(('leaf', 'sub')), may hold values from 0 to 255, as said below
- pair_count: int32 [256], P(('leaf', 'sub')), may hold values from 1 to 3, as said below
- pair_coupling: bfloat16 [256, 3, 128, 128], P(('leaf', 'sub')), may hold values from -0.3125 to 0.3125
- top_list: int32 [8, 2], P('leaf'), may hold values from 0 to 7, as said below
- top_coupling: bfloat16 [8, 2, 128, 128], P('leaf'), may hold values from -0.0625 to 0.0625
Outputs:
- product: float32 [1048576, 2, 128], P(('leaf', 'sub'))
Inputs may be any that keep to these rules, and one draw needn't show every extreme that they name: `order`: each row is a permutation. `near_list`: entry 0 of a leaf's list is the leaf itself; entries 1 and 2 are, in either order, the leaves just before and just after it in leaf order within its subtree; where one of them does not exist, the other stands in entry 1 and the leaf itself in entry 2. Only the first near_count entries of a list are used; they never repeat a leaf. Some leaf uses all 3. `pair_list`: the entries of a device node are distinct devices of its own subtree whose sub index differs from its own by 1 to 4. Only the first pair_count entries are used. Some device uses all 3. `top_list`: the entries of a subtree are distinct subtrees other than itself.
All inputs are finite; a program needn't handle non-finite values.
Results may differ from a plain program's by a relative error of at most 0.008.
Values may be sent and summed in bfloat16 or wider, within the bound.
No kernel may reach another device: no remote copies, remote signals or barrier semaphores. Data moves between devices by JAX's collectives and lax.ppermute only.
A program may use at most 64 MiB of HBM per device.

v0:
```python
import jax
import jax.numpy as jnp
from jax import lax
from jax.sharding import PartitionSpec as P

REACH = 4


exact_mode = lax.Precision.HIGHEST


def shifted(block, axis, distance):
    devices = range(lax.axis_size(axis))
    route = [(i - distance, i) for i in devices if i - distance in devices]
    return lax.ppermute(block, axis, route)


def gathered_total(array, axis):
    parts = lax.all_gather(array, axis)
    return parts.sum(axis=0)


def in_order(parts, dim):
    parts = jnp.moveaxis(parts, 0, dim)
    dims = parts.shape
    return parts.reshape(*dims[:dim], dims[dim] * dims[dim + 1], *dims[dim + 2 :])


def from_everyone(array, axis):
    peers = lax.axis_size(axis)
    return lax.all_to_all(
        jnp.broadcast_to(array[None], (peers, *array.shape)), axis, 0, 0, tiled=True
    )


def collect(array, axis, dim):
    return in_order(from_everyone(array, axis), dim)


def with_halo(array, sides, width):
    for axis, dim in sides:
        peers, length = (lax.axis_size(axis), array.shape[dim])
        up = [(i, (i + 1) % peers) for i in range(peers - 1)]
        down = [(j, i) for i, j in up]
        last = lax.slice_in_dim(array, length - width, length, axis=dim)
        first = lax.slice_in_dim(array, 0, width, axis=dim)
        before = lax.ppermute(last, axis, up)
        after = lax.ppermute(first, axis, down)
        array = jnp.concatenate([before, array, after], axis=dim)
    return array


def kernel_tile(rows_scaled, rows_sq, cols_scaled, cols_sq):
    cross = lax.dot_general(
        rows_scaled, cols_scaled, (((1,), (1,)), ((), ())), preferred_element_type=jnp.float32
    )
    distance = rows_sq[:, None] + cols_sq[None, :] - 2.0 * cross
    return jnp.exp(-0.5 * distance).astype(jnp.bfloat16)


def select_block(stack, index):
    return lax.dynamic_index_in_dim(stack, index, 0, keepdims=False)


def row_squares(values):
    return jnp.sum(jnp.square(values.astype(jnp.float32)), axis=-1)


def near_block(rows_scaled, rows_sq, links, used_count, offset_base, ext_scaled, ext_sq, ext_vals):

    def add_member(member, running):
        target = links[member] - offset_base
        tile = kernel_tile(
            rows_scaled, rows_sq, select_block(ext_scaled, target), select_block(ext_sq, target)
        )
        return running + jnp.dot(
            tile, select_block(ext_vals, target), preferred_element_type=jnp.float32
        )

    start_value = jnp.zeros((rows_scaled.shape[0], ext_vals.shape[2]), jnp.float32)
    return lax.fori_loop(jnp.int32(0), used_count, add_member, start_value)


def per_device(
    points,
    vectors,
    inv_length,
    order,
    leaf_basis,
    leaf_transfer,
    level_transfer,
    near_list,
    near_count,
    pair_list,
    pair_count,
    pair_coupling,
    top_list,
    top_coupling,
):
    sub_count = lax.axis_size("sub")
    levels_count = sub_count.bit_length() - 1
    sub_pos = lax.axis_index("sub")
    top_pos = lax.axis_index("leaf")
    dev_pos = top_pos * sub_count + sub_pos
    leaf_count, leaf_rows, coef_rank = leaf_basis.shape
    per_dev = leaf_count * leaf_rows
    features = points.shape[1]
    columns = vectors.shape[1] * vectors.shape[2]
    row_order = order[0]
    ordered = vectors.reshape(per_dev, columns)[row_order]
    scaled = (points[row_order].astype(jnp.float32) * inv_length[None, :]).astype(jnp.bfloat16)
    leaf_vals = ordered.reshape(leaf_count, leaf_rows, columns)
    leaf_scaled = scaled.reshape(leaf_count, leaf_rows, features)
    leaf_sq = row_squares(leaf_scaled)
    leaf_coef = jnp.einsum(
        "lpr,lpw->lrw", leaf_basis, leaf_vals, preferred_element_type=jnp.float32
    )
    node_coef = jnp.einsum(
        "lrs,lrw->sw", leaf_transfer.astype(jnp.float32), leaf_coef, precision=exact_mode
    )
    node_low = node_coef.astype(jnp.bfloat16)
    window_parts = []
    for slot in range(2 * REACH + 1):
        distance = REACH - slot
        if distance == 0:
            window_parts.append(node_low)
        else:
            window_parts.append(shifted(node_low, "sub", distance))
    window = jnp.stack(window_parts)
    pair_field = jnp.zeros((coef_rank, columns), jnp.float32)
    for member in range(pair_list.shape[1]):
        source = select_block(window, pair_list[0, member] - dev_pos + REACH)
        product_term = jnp.dot(pair_coupling[0, member], source, preferred_element_type=jnp.float32)
        pair_field = pair_field + jnp.where(member < pair_count[0], product_term, 0.0)
    level_table = level_transfer[0]
    matrices = []
    for depth_step in range(levels_count):
        first_node = 2 * sub_count - 2 * (sub_count >> depth_step)
        matrices.append(
            select_block(level_table, first_node + jnp.right_shift(sub_pos, depth_step)).astype(
                jnp.float32
            )
        )
    path_product = matrices[0]
    for depth_step in range(1, levels_count):
        path_product = jnp.dot(path_product, matrices[depth_step], precision=exact_mode)
    lifted = lax.dot_general(
        path_product, node_coef, (((0,), (0,)), ((), ())), precision=exact_mode
    )
    top_coef = gathered_total(lifted, "sub")
    top_low = top_coef.astype(jnp.bfloat16)
    sources = collect(top_low[None], "leaf", 0)
    top_field = jnp.zeros((coef_rank, columns), jnp.float32)
    for member in range(top_list.shape[1]):
        top_field = top_field + jnp.dot(
            top_coupling[0, member],
            select_block(sources, top_list[0, member]),
            preferred_element_type=jnp.float32,
        )
    node_field = jnp.dot(path_product, top_field, precision=exact_mode)
    node_field = node_field + pair_field
    leaf_field = jnp.einsum(
        "lrs,sw->lrw", leaf_transfer.astype(jnp.float32), node_field, precision=exact_mode
    ).astype(jnp.bfloat16)
    far_sum = jnp.einsum("lpr,lrw->lpw", leaf_basis, leaf_field, preferred_element_type=jnp.float32)
    packed = jnp.concatenate(
        [
            leaf_scaled.reshape(leaf_count, leaf_rows * features),
            leaf_vals.reshape(leaf_count, leaf_rows * columns),
        ],
        axis=1,
    )
    framed = with_halo(packed, (("sub", 0),), 1)
    ext_scaled = framed[:, : leaf_rows * features].reshape(leaf_count + 2, leaf_rows, features)
    ext_vals = framed[:, leaf_rows * features :].reshape(leaf_count + 2, leaf_rows, columns)
    ext_sq = row_squares(ext_scaled)
    offset_base = dev_pos * leaf_count - 1
    near_parts = []
    for leaf_index in range(leaf_count):
        near_parts.append(
            near_block(
                leaf_scaled[leaf_index],
                leaf_sq[leaf_index],
                near_list[leaf_index],
                near_count[leaf_index],
                offset_base,
                ext_scaled,
                ext_sq,
                ext_vals,
            )
        )
    near_sum = jnp.stack(near_parts)
    leaf_sum = (far_sum + near_sum).reshape(per_dev, columns)
    result = jnp.zeros((per_dev, columns), jnp.float32).at[row_order].set(leaf_sum)
    return result.reshape(per_dev, vectors.shape[1], vectors.shape[2])


def solution(mesh):
    return jax.shard_map(
        per_device,
        mesh=mesh,
        in_specs=(
            P(("leaf", "sub"), None),
            P(("leaf", "sub"), None, None),
            P(),
            P(("leaf", "sub"), None),
            P(("leaf", "sub"), None, None),
            P(("leaf", "sub"), None, None),
            P("leaf", None, None, None),
            P(("leaf", "sub"), None),
            P(("leaf", "sub")),
            P(("leaf", "sub"), None),
            P(("leaf", "sub")),
            P(("leaf", "sub"), None, None, None),
            P("leaf", None),
            P("leaf", None, None, None),
        ),
        out_specs=P(("leaf", "sub"), None, None),
        check_vma=False,
    )
```

profile of v0, /device:TPU:102, one launch (start us, length us, event | category | flops | bytes accessed | tf_op | source)
XLA Modules:
  0.0 340.2 jit_solution(6462270961313579487)
XLA Ops:
  8.0 3.2 copy.37
  11.2 17.9 %gather_fusion = bf16[4096,256]{1,0:T(8,128)(2,1)} fusion(bf16[4096,256]{1,0:T(8,128)(2,1)} %bitcast.458, s32[4096]{0:T(1024)S(1)} %broadcast_clamp_fusion), kind=kCustom, calls=%fused_computation | custom fusion | bytes 4210688 | tf_op jit(solution)/shard_map/gather | solution.py:110
  29.1 2.4 convolution_bitcast_fusion
  32.8 6.4 %collective-permute-start = (bf16[128,256]{0,1:T(8,128)(2,1)}, bf16[128,256]{0,1:T(8,128)(2,1)}, u32[]{:S(2)}, u32[]{:S(2)}) collective-permute-start(bf16[128,256]{0,1:T(8,128)(2,1)} %convert_bitcast_fusion), channel_id=1, source_target_pairs={{0,4},{1,5},{2,6},{3,7},{4,8},{5,9},{6,10},{7,11},{8,12},{9,13},{1... | collective-permute-start | bytes 196616 | tf_op jit(solution)/shard_map/ppermute | solution.py:15
  39.2 1.9 collective-permute-start.1
  41.2 1.9 collective-permute-start.2
  45.0 3.9 %collective-permute-start.4 = (bf16[128,256]{0,1:T(8,128)(2,1)}, bf16[128,256]{0,1:T(8,128)(2,1)}, u32[]{:S(2)}, u32[]{:S(2)}) collective-permute-start(bf16[128,256]{0,1:T(8,128)(2,1)} %convert_bitcast_fusion), channel_id=1, source_target_pairs={{1,0},{2,1},{3,2},{4,3},{5,4},{6,5},{7,6},{8,7},{9,8},{10,9},{11,1... | collective-permute-start | bytes 196616 | tf_op jit(solution)/shard_map/ppermute | solution.py:15
  56.2 3.9 %reshape_reshape.4 = bf16[8,131072]{1,0:T(8,128)(2,1)} reshape(bf16[4096,256]{1,0:T(8,128)(2,1)} %gather_fusion) | data formatting | bytes 4194304 | tf_op jit(solution)/shard_map/reshape;reshape | solution.py:169
  61.3 12.1 %gather_fusion.1 = bf16[4096,32]{1,0:T(8,128)(2,1)S(1)} fusion(bf16[4096,32]{1,0:T(8,128)(2,1)S(1)} %copy.24, s32[4096]{0:T(1024)S(1)} %broadcast_clamp_fusion), kind=kCustom, calls=%fused_computation.1 | custom fusion | bytes 540672 | tf_op jit(solution)/shard_map/gather | solution.py:111
  79.3 3.7 %pad_maximum_fusion.4 = (bf16[1,147456]{1,0:T(2,128)(2,1)S(1)}, bf16[1,147456]{1,0:T(2,128)(2,1)S(1)}) fusion(bf16[8,131072]{1,0:T(8,128)(2,1)} %reshape_reshape.4, bf16[8,16384]{1,0:T(8,128)(2,1)S(1)} %multiply_convert_fusion.1), kind=kLoop, calls=%fused_computation.195 | loop fusion | flops 1179648 | bytes 2949120 | tf_op jit(solution)/shard_map/slice | solution.py:45
  83.8 4.8 %collective-permute-start.5 = (bf16[128,256]{0,1:T(8,128)(2,1)}, bf16[128,256]{0,1:T(8,128)(2,1)S(1)}, u32[]{:S(2)}, u32[]{:S(2)}) collective-permute-start(bf16[128,256]{0,1:T(8,128)(2,1)} %convert_bitcast_fusion), channel_id=1, source_target_pairs={{2,0},{3,1},{4,2},{5,3},{6,4},{7,5},{8,6},{9,7},{10,8},{11,9},{12,... | collective-permute-start | bytes 196616 | tf_op jit(solution)/shard_map/ppermute | solution.py:15
  89.4 7.8 %collective-permute-start.6 = (bf16[128,256]{0,1:T(8,128)(2,1)}, bf16[128,256]{0,1:T(8,128)(2,1)S(1)}, u32[]{:S(2)}, u32[]{:S(2)}) collective-permute-start(bf16[128,256]{0,1:T(8,128)(2,1)} %convert_bitcast_fusion), channel_id=1, source_target_pairs={{3,0},{4,1},{5,2},{6,3},{7,4},{8,5},{9,6},{10,7},{11,8},{12,9},{13... | collective-permute-start | bytes 196616 | tf_op jit(solution)/shard_map/ppermute | solution.py:15
  98.1 4.5 %collective-permute-start.7 = (bf16[128,256]{0,1:T(8,128)(2,1)}, bf16[128,256]{0,1:T(8,128)(2,1)S(1)}, u32[]{:S(2)}, u32[]{:S(2)}) collective-permute-start(bf16[128,256]{0,1:T(8,128)(2,1)} %convert_bitcast_fusion), channel_id=1, source_target_pairs={{4,0},{5,1},{6,2},{7,3},{8,4},{9,5},{10,6},{11,7},{12,8},{13,9},{1... | collective-permute-start | bytes 196616 | tf_op jit(solution)/shard_map/ppermute | solution.py:15
  103.4 5.1 %collective-permute-start.8 = (bf16[1,147456]{1,0:T(2,128)(2,1)S(1)}, bf16[1,147456]{1,0:T(2,128)(2,1)S(1)}, u32[]{:S(2)}, u32[]{:S(2)}) collective-permute-start(bf16[1,147456]{1,0:T(2,128)(2,1)S(1)} %get-tuple-element.607), channel_id=1, source_target_pairs={{0,1},{1,2},{2,3},{3,4},{4,5},{5,6},{6,7},{7,8},{8,9},{9,10},{10,1... | collective-permute-start | bytes 884744 | tf_op jit(solution)/shard_map/ppermute | solution.py:47
  109.5 2.1 collective-permute-start.9
  113.8 20.0 %collective-permute-done.8 = bf16[1,147456]{1,0:T(2,128)(2,1)S(1)} collective-permute-done((bf16[1,147456]{1,0:T(2,128)(2,1)S(1)}, bf16[1,147456]{1,0:T(2,128)(2,1)S(1)}, u32[]{:S(2)}, u32[]{:S(2)}) %collective-permute-start.8) | collective-permute-done | bytes 294944 | tf_op jit(solution)/shard_map/ppermute | solution.py:47
  133.9 5.2 %collective-permute-done.9 = bf16[1,147456]{1,0:T(2,128)(2,1)S(1)} collective-permute-done((bf16[1,147456]{1,0:T(2,128)(2,1)S(1)}, bf16[1,147456]{1,0:T(2,128)(2,1)S(1)}, u32[]{:S(2)}, u32[]{:S(2)}) %collective-permute-start.9) | collective-permute-done | bytes 294944 | tf_op jit(solution)/shard_map/ppermute | solution.py:48
  140.1 2.1 reshape.119
  142.9 3.3 pad_maximum_fusion
  148.9 8.7 %while.81 = (s32[]{:T(128)}, f32[512,256]{1,0:T(8,128)S(1)}, s32[]{:T(128)}, f32[1,512]{1,0:T(1,128)S(1)}, s32[3]{0:T(128)}, /*index=5*/s32[]{:T(128)}, f32[10,5...) while((s32[]{:T(128)}, f32[512,256]{1,0:T(8,128)S(1)}, ...), condition=%wide.region_6.7_spmd, body=%wide.region_5.6_spmd.sunk | while | flops 152436736 | bytes 1582309 | solution.py:81
  157.9 8.6 %while.80 = (s32[]{:T(128)}, f32[512,256]{1,0:T(8,128)S(1)}, s32[]{:T(128)}, f32[1,512]{1,0:T(1,128)S(1)}, s32[3]{0:T(128)}, /*index=5*/s32[]{:T(128)}, f32[10,5...) while((s32[]{:T(128)}, f32[512,256]{1,0:T(8,128)S(1)}, ...), condition=%wide.region_4.5_spmd, body=%wide.region_3.4_spmd.sunk | while | flops 152436736 | bytes 1582309 | solution.py:81
  166.8 7.8 %while.82 = (s32[]{:T(128)}, f32[512,256]{1,0:T(8,128)S(1)}, s32[]{:T(128)}, f32[1,512]{1,0:T(1,128)S(1)}, s32[3]{0:T(128)S(1)}, /*index=5*/s32[]{:T(128)}, f32[...) while((s32[]{:T(128)}, f32[512,256]{1,0:T(8,128)S(1)}, ...), condition=%wide.region_8.9_spmd, body=%wide.region_7.8_spmd.sunk | while | flops 152436736 | bytes 1582309 | solution.py:81
  177.5 9.3 %while.83 = (s32[]{:T(128)}, f32[512,256]{1,0:T(8,128)}, s32[]{:T(128)}, f32[1,512]{1,0:T(1,128)S(1)}, s32[3]{0:T(128)S(1)}, /*index=5*/s32[]{:T(128)}, f32[10,5...) while((s32[]{:T(128)}, f32[512,256]{1,0:T(8,128)}, ...), condition=%wide.region_10.11_spmd, body=%wide.region_9.10_spmd.sunk | while | flops 152436736 | bytes 1582309 | solution.py:81
  179.4 2.5 fusion.303
  183.7 2.5 fusion.303
  186.9 2.0 copy.28
  189.8 14.7 %while.84 = (s32[]{:T(128)}, f32[512,256]{1,0:T(8,128)}, s32[]{:T(128)}, f32[1,512]{1,0:T(1,128)S(1)}, s32[3]{0:T(128)S(1)}, /*index=5*/s32[]{:T(128)}, f32[10,5...) while((s32[]{:T(128)}, f32[512,256]{1,0:T(8,128)}, ...), condition=%wide.region_12.13_spmd, body=%wide.region_11.12_spmd.sunk | while | flops 152436736 | bytes 1582309 | solution.py:81
  191.9 2.5 fusion.307
  196.5 2.5 fusion.307
  201.2 2.5 fusion.307
  204.4 2.1 copy.29
  207.3 9.5 %while.85 = (s32[]{:T(128)}, f32[512,256]{1,0:T(8,128)}, s32[]{:T(128)}, f32[1,512]{1,0:T(1,128)S(1)}, s32[3]{0:T(128)S(1)}, /*index=5*/s32[]{:T(128)}, f32[10,5...) while((s32[]{:T(128)}, f32[512,256]{1,0:T(8,128)}, ...), condition=%wide.region_14.15_spmd, body=%wide.region_13.14_spmd.sunk | while | flops 152436736 | bytes 1582309 | solution.py:81
  209.3 2.5 fusion.311
  213.8 2.5 fusion.311
  216.9 2.0 copy.30
  219.8 5.2 %while.86 = (s32[]{:T(128)}, f32[512,256]{1,0:T(8,128)}, s32[]{:T(128)}, f32[1,512]{1,0:T(1,128)S(1)}, s32[3]{0:T(128)S(1)}, /*index=5*/s32[]{:T(128)}, f32[10,5...) while((s32[]{:T(128)}, f32[512,256]{1,0:T(8,128)}, ...), condition=%wide.region_16.17_spmd, body=%wide.region_15.16_spmd.sunk | while | flops 152436736 | bytes 1582309 | solution.py:81
  221.7 2.6 fusion.315
  225.0 2.1 copy.31
  227.8 5.0 %while.87 = (s32[]{:T(128)}, f32[512,256]{1,0:T(8,128)}, s32[]{:T(128)}, f32[1,512]{1,0:T(1,128)S(1)}, s32[3]{0:T(128)S(1)}, /*index=5*/s32[]{:T(128)}, f32[10,5...) while((s32[]{:T(128)}, f32[512,256]{1,0:T(8,128)}, ...), condition=%wide.region_18.19_spmd, body=%wide.region_17.18_spmd.sunk | while | flops 152436736 | bytes 1582309 | solution.py:81
  229.7 2.5 fusion.319
  232.9 2.1 copy.32
  240.0 2.5 reduce_sum.27
  243.4 42.1 %all-to-all-start = ((bf16[8,1,128,256]{3,2,1,0:T(8,128)(2,1)}), bf16[8,1,128,256]{3,2,1,0:T(8,128)(2,1)S(1)}, u32[]{:S(2)}, u32[]{:S(2)}) async-start(bf16[8,1,128,256]{3,2,1,0:T(8,128)(2,1)} %broadcast_in_dim.13), calls=%async_computation | async-start | bytes 1048576 | tf_op jit(solution)/shard_map/all_to_all | solution.py:31
  287.1 8.6 %all-to-all-done = bf16[8,1,128,256]{3,2,1,0:T(8,128)(2,1)S(1)} async-done(((bf16[8,1,128,256]{3,2,1,0:T(8,128)(2,1)}), bf16[8,1,128,256]{3,2,1,0:T(8,128)(2,1)S(1)}, u32[]{:S(2)}, u32[]{:S(2)}) %all-to-all-start) | async-done | bytes 524320 | tf_op jit(solution)/shard_map/all_to_all | solution.py:31
  297.1 4.9 %bitcast_add_fusion = f32[8,512,256]{1,2,0:T(8,128)} fusion(f32[8,512,256]{1,2,0:T(8,128)} %bitcast_dynamic-update-slice_fusion, bf16[8,128,256]{1,2,0:T(8,128)(2,1)S(1)} %fusion.178, bf16[8,512,128]{2,1,0:T(8,128)(2,1)S(1)} %copy-done.3), kind=kOutput, calls=%fused_computation.174 | convolution fusion | flops 269484032 | bytes 9961472 | tf_op jit(solution)/shard_map/lpr,lrw->lpw/dot_general | solution.py:165
  302.0 5.3 %copy.33 = f32[8,512,256]{2,1,0:T(8,128)} copy(f32[8,512,256]{1,2,0:T(8,128)} %bitcast_add_fusion) | data formatting | bytes 8388608 | tf_op jit(solution)/shard_map/add | solution.py:193
  307.4 20.2 %scatter_custom_fusion = f32[4096,256]{1,0:T(8,128)} fusion(s32[4096]{0:T(1024)} %bitcast.466, f32[4096,256]{1,0:T(8,128)} %bitcast.463, f32[]{:T(128)} %constant.207.clone.1), kind=kCustom, calls=%fused_computation.179 | custom fusion | bytes 4194816 | tf_op jit(solution)/shard_map/scatter | solution.py:194
  327.6 5.7 %reshape.122 = f32[4096,2,128]{2,1,0:T(2,128)} reshape(f32[4096,256]{1,0:T(8,128)} %scatter_custom_fusion) | data formatting | bytes 8388608 | tf_op jit(solution)/shard_map/reshape | solution.py:195
  (165 shorter events, 59.9 us)
Async XLA Ops:
  6.5 42.4 %copy-start = (bf16[1,62,128,128]{3,2,1,0:T(8,128)(2,1)S(1)}, bf16[1,62,128,128]{3,2,1,0:T(8,128)(2,1)}, u32[]{:S(2)}) copy-start(bf16[1,62,128,128]{3,2,1,0:T(8,128)(2,1)} %param.36) | copy-start | bytes 6094852
  6.5 233.5 %all-gather.3.cloned.1.call-start = ((), (), s32[]{:S(2)}) async-start(), calls=%async_computation.1 | async-start | bytes 4325376 | tf_op jit(solution)/shard_map/all_gather | solution.py:19
  7.4 0.6 copy-start.19
  11.2 17.9 %copy-start.2 = (bf16[8,512,128]{2,1,0:T(8,128)(2,1)S(1)}, bf16[8,512,128]{2,1,0:T(8,128)(2,1)}, u32[]{:S(2)}) copy-start(bf16[8,512,128]{2,1,0:T(8,128)(2,1)} %param.34) | copy-start | bytes 3145732
  29.1 2.4 copy-start.11
  31.5 19.1 %copy-start.22 = (s32[1,3]{1,0:T(1,128)S(1)}, s32[1,3]{1,0:T(1,128)}, u32[]{:S(2)}) copy-start(s32[1,3]{1,0:T(1,128)} %param.39) | copy-start | bytes 40
  31.6 21.5 %copy-start.24 = (s32[1,2]{1,0:T(1,128)S(1)}, s32[1,2]{1,0:T(1,128)}, u32[]{:S(2)}) copy-start(s32[1,2]{1,0:T(1,128)} %param.42) | copy-start | bytes 28
  32.8 50.9 %collective-permute-start = (bf16[128,256]{0,1:T(8,128)(2,1)}, bf16[128,256]{0,1:T(8,128)(2,1)}, u32[]{:S(2)}, u32[]{:S(2)}) collective-permute-start(bf16[128,256]{0,1:T(8,128)(2,1)} %convert_bitcast_fusion), channel_id=1, source_target_pairs={{0,4},{1,5},{2,6},{3,7},{4,8},{5,9},{6,10},{7,11},{8,12},{9,13},{1... | collective-permute-start | bytes 196616 | tf_op jit(solution)/shard_map/ppermute | solution.py:15
  39.2 50.2 %collective-permute-start.1 = (bf16[128,256]{0,1:T(8,128)(2,1)}, bf16[128,256]{0,1:T(8,128)(2,1)}, u32[]{:S(2)}, u32[]{:S(2)}) collective-permute-start(bf16[128,256]{0,1:T(8,128)(2,1)} %convert_bitcast_fusion), channel_id=1, source_target_pairs={{0,3},{1,4},{2,5},{3,6},{4,7},{5,8},{6,9},{7,10},{8,11},{9,12},{10... | collective-permute-start | bytes 196616 | tf_op jit(solution)/shard_map/ppermute | solution.py:15
  41.2 57.0 %collective-permute-start.2 = (bf16[128,256]{0,1:T(8,128)(2,1)}, bf16[128,256]{0,1:T(8,128)(2,1)}, u32[]{:S(2)}, u32[]{:S(2)}) collective-permute-start(bf16[128,256]{0,1:T(8,128)(2,1)} %convert_bitcast_fusion), channel_id=1, source_target_pairs={{0,2},{1,3},{2,4},{3,5},{4,6},{5,7},{6,8},{7,9},{8,10},{9,11},{10,... | collective-permute-start | bytes 196616 | tf_op jit(solution)/shard_map/ppermute | solution.py:15
  43.1 60.4 %collective-permute-start.3 = (bf16[128,256]{0,1:T(8,128)(2,1)}, bf16[128,256]{0,1:T(8,128)(2,1)}, u32[]{:S(2)}, u32[]{:S(2)}) collective-permute-start(bf16[128,256]{0,1:T(8,128)(2,1)} %convert_bitcast_fusion), channel_id=1, source_target_pairs={{0,1},{1,2},{2,3},{3,4},{4,5},{5,6},{6,7},{7,8},{8,9},{9,10},{10,1... | collective-permute-start | bytes 196616 | tf_op jit(solution)/shard_map/ppermute | solution.py:15
  45.0 64.5 %collective-permute-start.4 = (bf16[128,256]{0,1:T(8,128)(2,1)}, bf16[128,256]{0,1:T(8,128)(2,1)}, u32[]{:S(2)}, u32[]{:S(2)}) collective-permute-start(bf16[128,256]{0,1:T(8,128)(2,1)} %convert_bitcast_fusion), channel_id=1, source_target_pairs={{1,0},{2,1},{3,2},{4,3},{5,4},{6,5},{7,6},{8,7},{9,8},{10,9},{11,1... | collective-permute-start | bytes 196616 | tf_op jit(solution)/shard_map/ppermute | solution.py:15
  49.1 11.7 %copy-start.12 = (bf16[4096,32]{0,1:T(8,128)(2,1)S(1)}, bf16[4096,32]{0,1:T(8,128)(2,1)}, u32[]{:S(2)}) copy-start(bf16[4096,32]{0,1:T(8,128)(2,1)} %param.30) | copy-start | bytes 786436
  61.3 14.0 %copy-start.23 = (f32[32]{0:T(128)S(1)}, f32[32]{0:T(128)}, u32[]{:S(2)}) copy-start(f32[32]{0:T(128)} %param.32) | copy-start | bytes 388
  75.3 1.8 copy-start.17
  75.9 3.3 copy-start.4
  77.1 6.0 %copy-start.21 = (s32[8]{0:T(128)S(1)}, s32[8]{0:T(128)}, u32[]{:S(2)}) copy-start(s32[8]{0:T(128)} %param.38) | copy-start | bytes 100
  79.2 33.3 %copy-start.18 = (bf16[1,3,128,128]{3,2,1,0:T(8,128)(2,1)S(1)}, bf16[1,3,128,128]{3,2,1,0:T(8,128)(2,1)}, u32[]{:S(2)}) copy-start(bf16[1,3,128,128]{3,2,1,0:T(8,128)(2,1)} %param.41) | copy-start | bytes 294916
  83.8 28.7 %collective-permute-start.5 = (bf16[128,256]{0,1:T(8,128)(2,1)}, bf16[128,256]{0,1:T(8,128)(2,1)S(1)}, u32[]{:S(2)}, u32[]{:S(2)}) collective-permute-start(bf16[128,256]{0,1:T(8,128)(2,1)} %convert_bitcast_fusion), channel_id=1, source_target_pairs={{2,0},{3,1},{4,2},{5,3},{6,4},{7,5},{8,6},{9,7},{10,8},{11,9},{12,... | collective-permute-start | bytes 196616 | tf_op jit(solution)/shard_map/ppermute | solution.py:15
  89.4 23.0 %collective-permute-start.6 = (bf16[128,256]{0,1:T(8,128)(2,1)}, bf16[128,256]{0,1:T(8,128)(2,1)S(1)}, u32[]{:S(2)}, u32[]{:S(2)}) collective-permute-start(bf16[128,256]{0,1:T(8,128)(2,1)} %convert_bitcast_fusion), channel_id=1, source_target_pairs={{3,0},{4,1},{5,2},{6,3},{7,4},{8,5},{9,6},{10,7},{11,8},{12,9},{13... | collective-permute-start | bytes 196616 | tf_op jit(solution)/shard_map/ppermute | solution.py:15
  98.1 14.4 %collective-permute-start.7 = (bf16[128,256]{0,1:T(8,128)(2,1)}, bf16[128,256]{0,1:T(8,128)(2,1)S(1)}, u32[]{:S(2)}, u32[]{:S(2)}) collective-permute-start(bf16[128,256]{0,1:T(8,128)(2,1)} %convert_bitcast_fusion), channel_id=1, source_target_pairs={{4,0},{5,1},{6,2},{7,3},{8,4},{9,5},{10,6},{11,7},{12,8},{13,9},{1... | collective-permute-start | bytes 196616 | tf_op jit(solution)/shard_map/ppermute | solution.py:15
  103.4 30.4 %collective-permute-start.8 = (bf16[1,147456]{1,0:T(2,128)(2,1)S(1)}, bf16[1,147456]{1,0:T(2,128)(2,1)S(1)}, u32[]{:S(2)}, u32[]{:S(2)}) collective-permute-start(bf16[1,147456]{1,0:T(2,128)(2,1)S(1)} %get-tuple-element.607), channel_id=1, source_target_pairs={{0,1},{1,2},{2,3},{3,4},{4,5},{5,6},{6,7},{7,8},{8,9},{9,10},{10,1... | collective-permute-start | bytes 884744 | tf_op jit(solution)/shard_map/ppermute | solution.py:47
  109.5 29.6 %collective-permute-start.9 = (bf16[1,147456]{1,0:T(2,128)(2,1)S(1)}, bf16[1,147456]{1,0:T(2,128)(2,1)S(1)}, u32[]{:S(2)}, u32[]{:S(2)}) collective-permute-start(bf16[1,147456]{1,0:T(2,128)(2,1)S(1)} %get-tuple-element.608), channel_id=1, source_target_pairs={{1,0},{2,1},{3,2},{4,3},{5,4},{6,5},{7,6},{8,7},{9,8},{10,9},{11,1... | collective-permute-start | bytes 884744 | tf_op jit(solution)/shard_map/ppermute | solution.py:48
  148.9 9.0 %copy-start.16 = (bf16[512,32]{1,0:T(8,128)(2,1)S(1)}, bf16[512,32]{1,0:T(8,128)(2,1)}, u32[]{:S(2)}) copy-start(bf16[512,32]{1,0:T(8,128)(2,1)} %get-tuple-element.1142) | copy-start | bytes 98308
  157.9 8.9 %copy-start.27 = (s32[3]{0:T(128)S(1)}, s32[3]{0:T(128)}, u32[]{:S(2)}) copy-start(s32[3]{0:T(128)} %get-tuple-element.1222) | copy-start | bytes 40
  166.8 10.8 %copy-start.15 = (bf16[512,32]{1,0:T(8,128)(2,1)S(1)}, bf16[512,32]{1,0:T(8,128)(2,1)}, u32[]{:S(2)}) copy-start(bf16[512,32]{1,0:T(8,128)(2,1)} %get-tuple-element.1268) | copy-start | bytes 98308
  166.8 10.7 %copy-start.26 = (s32[3]{0:T(128)S(1)}, s32[3]{0:T(128)}, u32[]{:S(2)}) copy-start(s32[3]{0:T(128)} %get-tuple-element.1264) | copy-start | bytes 40
  174.6 0.8 copy-start.10
  177.5 12.2 %copy-start.25 = (s32[3]{0:T(128)S(1)}, s32[3]{0:T(128)}, u32[]{:S(2)}) copy-start(s32[3]{0:T(128)} %get-tuple-element.1306) | copy-start | bytes 40
  189.8 17.6 %copy-start.14 = (bf16[512,32]{1,0:T(8,128)(2,1)S(1)}, bf16[512,32]{1,0:T(8,128)(2,1)}, u32[]{:S(2)}) copy-start(bf16[512,32]{1,0:T(8,128)(2,1)} %get-tuple-element.1352) | copy-start | bytes 98308
  219.8 8.1 %copy-start.13 = (bf16[512,32]{1,0:T(8,128)(2,1)S(1)}, bf16[512,32]{1,0:T(8,128)(2,1)}, u32[]{:S(2)}) copy-start(bf16[512,32]{1,0:T(8,128)(2,1)} %get-tuple-element.1436) | copy-start | bytes 98308
  232.8 4.6 %copy-start.5 = (f32[512,256]{0,1:T(8,128)S(1)}, f32[512,256]{0,1:T(8,128)}, u32[]{:S(2)}) copy-start(f32[512,256]{0,1:T(8,128)} %copy.28) | copy-start | bytes 1572868
  232.9 5.5 %copy-start.6 = (f32[512,256]{0,1:T(8,128)S(1)}, f32[512,256]{0,1:T(8,128)}, u32[]{:S(2)}) copy-start(f32[512,256]{0,1:T(8,128)} %copy.29) | copy-start | bytes 1572868
  235.0 4.2 %copy-start.7 = (f32[512,256]{0,1:T(8,128)S(1)}, f32[512,256]{0,1:T(8,128)}, u32[]{:S(2)}) copy-start(f32[512,256]{0,1:T(8,128)} %copy.30) | copy-start | bytes 1572868
  240.0 45.5 %copy-start.8 = (f32[512,256]{0,1:T(8,128)S(1)}, f32[512,256]{0,1:T(8,128)}, u32[]{:S(2)}) copy-start(f32[512,256]{0,1:T(8,128)} %copy.31) | copy-start | bytes 1572868
  240.0 46.3 %copy-start.9 = (f32[512,256]{0,1:T(8,128)S(1)}, f32[512,256]{0,1:T(8,128)}, u32[]{:S(2)}) copy-start(f32[512,256]{0,1:T(8,128)} %copy.32) | copy-start | bytes 1572868
  242.5 53.3 %copy-start.20 = (bf16[1,2,128,128]{3,2,1,0:T(8,128)(2,1)S(1)}, bf16[1,2,128,128]{3,2,1,0:T(8,128)(2,1)}, u32[]{:S(2)}) copy-start(bf16[1,2,128,128]{3,2,1,0:T(8,128)(2,1)} %param.43) | copy-start | bytes 196612
  243.4 53.7 %copy-start.3 = (bf16[8,512,128]{2,1,0:T(8,128)(2,1)S(1)}, bf16[8,512,128]{2,1,0:T(8,128)(2,1)}, u32[]{:S(2)}) copy-start(bf16[8,512,128]{2,1,0:T(8,128)(2,1)} %param.34) | copy-start | bytes 3145732
  243.4 52.4 %all-to-all-start = ((bf16[8,1,128,256]{3,2,1,0:T(8,128)(2,1)}), bf16[8,1,128,256]{3,2,1,0:T(8,128)(2,1)S(1)}, u32[]{:S(2)}, u32[]{:S(2)}) async-start(bf16[8,1,128,256]{3,2,1,0:T(8,128)(2,1)} %broadcast_in_dim.13), calls=%async_computation | async-start | bytes 1048576 | tf_op jit(solution)/shard_map/all_to_all | solution.py:31
  307.4 25.9 %copy-start.1 = (bf16[1,62,128,128]{3,2,1,0:T(8,128)(2,1)S(1)}, bf16[1,62,128,128]{3,2,1,0:T(8,128)(2,1)}, u32[]{:S(2)}) copy-start(bf16[1,62,128,128]{3,2,1,0:T(8,128)(2,1)} %param.36) | copy-start | bytes 6094852
Sparse Core Ops, SparseCore 0:
  50.8 91.9 all-gather.2
where the time goes:
time: 344 us; the launch traced here: 340 us
  local copies, waits for them, and re-layouts  121 us (35%)
  starting transfers between devices  82.5 us (24%)
  matrix products  44 us (13%)
  waiting for transfers between devices  33.9 us (10%)
  loops' own time  25.1 us (7%)
  between operations  20.4 us (6%)
  other arithmetic  13.6 us (4%)
    all_to_all x1, starting transfers between devices, from_everyone(): lax.all_to_all(jnp.broadcast_to(array[None], (peers, *array.shape)), axis...  42.1 us
    ppermute x8, starting transfers between devices, shifted(): return lax.ppermute(block, axis, route)  33.2 us
    dot_general x15, matrix products, add_member(): jnp.dot(tile, select_block(ext_vals, target), preferred_element_type=jnp....  31.9 us
    another operation x8, loops' own time, near_block(): return lax.fori_loop(jnp.int32(0), used_count, add_member, start_value)  25.1 us
    scatter x1, local copies, waits for them, and re-layouts, per_device(): jnp.zeros((per_dev, columns), jnp.float32).at[row_order].set(leaf_sum)  20.2 us
    ppermute x1, waiting for transfers between devices, with_halo(): before = lax.ppermute(last, axis, up)  20 us
    gather x1, local copies, waits for them, and re-layouts, per_device(): ordered = vectors.reshape(per_dev, columns)[row_order]  17.9 us
    unnamed x73, local copies, waits for them, and re-layouts  16.2 us
  transfers between devices with their start and end apart: 12, of which 3 were waited for; matrix products, arithmetic and copies ran while one was open for 32% of the time, Pallas kernels for 0%

commit v1 on v0

v1 whole, which is shorter than its diff:
```python
import functools

import jax
import jax.numpy as jnp
from jax import lax
from jax.experimental import pallas as pl
from jax.experimental.pallas import tpu as pltpu
from jax.sharding import PartitionSpec as P

REACH = 4
LANES = 128
SUBLANES = 8
VMEM_LIMIT = 60 << 20
UNROLL = 32

bf16 = jnp.bfloat16
f32 = jnp.float32
exact_mode = lax.Precision.HIGHEST

SMEM_SPEC = pl.BlockSpec(memory_space=pltpu.SMEM)
VMEM_SPEC = pl.BlockSpec(memory_space=pltpu.VMEM)


def tn_dot(a, b, precision=None):
    return lax.dot_general(
        a, b, (((0,), (0,)), ((), ())), preferred_element_type=f32, precision=precision
    )


def nt_dot(a, b):
    return lax.dot_general(a, b, (((1,), (1,)), ((), ())), preferred_element_type=f32)


def nn_dot(a, b, precision=None):
    return lax.dot_general(
        a, b, (((1,), (0,)), ((), ())), preferred_element_type=f32, precision=precision
    )


def high_low(x):
    high = x.astype(bf16)
    return high, (x - high.astype(f32)).astype(bf16)


def row_loop(rows, step):
    def several(i, carry):
        for k in range(UNROLL):
            step(i * UNROLL + k)
        return carry

    lax.fori_loop(0, rows // UNROLL, several, 0)


def chunk_loop(rows, size, step):
    def one(i, carry):
        step(pl.ds(pl.multiple_of(i * size, size), size), i)
        return carry

    lax.fori_loop(0, rows // size, one, 0)


def gather_kernel(
    order,
    wanted,
    vectors,
    points,
    inv_length,
    basis,
    transfer,
    m0,
    m1,
    m2,
    m3,
    m4,
    vals_cols,
    rows_aug,
    send,
    path,
    table,
    held_vals,
    held_points,
):
    leaves, leaf_rows, rank = basis.shape
    per_dev, features = points.shape
    width = vectors.shape[1] * vectors.shape[2]

    lane = lax.broadcasted_iota(jnp.int32, (1, LANES), 1)
    is_feature = lane < features
    piece = lane - features
    first, second, third = [(piece == k) | (piece == k + 3) for k in range(3)]

    def augment(r, i):
        x = (points[r, :].astype(f32) * inv_length[...]).astype(bf16).astype(f32)
        table[r, 0:features] = x
        half = -0.5 * jnp.sum(x * x, axis=1, keepdims=True)
        h1 = half.astype(bf16).astype(f32)
        h2 = (half - h1).astype(bf16).astype(f32)
        h3 = half - h1 - h2
        extra = jnp.where(first, h1, jnp.where(second, h2, jnp.where(third, h3, 0.0)))
        table[r, :] = jnp.where(is_feature, table[r, :], extra)

    chunk_loop(per_dev, 256, augment)

    def move(p):
        source = order[0, p]
        held_vals[p] = vectors[source]
        held_points[pl.ds(p, 1), :] = table[pl.ds(source, 1), :]

    row_loop(per_dev, move)

    ones_left = (piece >= 0) & (piece < 3)
    ones_right = (piece >= 3) & (piece < 6)
    node = jnp.zeros((rank, width), f32)
    for leaf in range(leaves):
        base = leaf * leaf_rows

        def spread(r, i):
            start = pl.multiple_of(base + i * 64, 64)
            vals_cols[leaf, r, 0:width] = held_vals[pl.ds(start, 64)].reshape(64, width)
            got = held_points[pl.ds(start, 64), :]
            vals_cols[leaf, r, width : width + LANES] = jnp.where(ones_left, 1.0, got).astype(bf16)
            rows_aug[leaf, r, :] = jnp.where(ones_right, 1.0, got).astype(bf16)

        chunk_loop(leaf_rows, 64, spread)
        coef = tn_dot(basis[leaf], vals_cols[leaf, :, 0:width])
        high, low = high_low(coef)
        node = node + tn_dot(transfer[leaf], high) + tn_dot(transfer[leaf], low)

    product = m0[0, 0].astype(f32)
    for m in (m1, m2, m3, m4):
        product = nn_dot(product, m[0, 0].astype(f32), exact_mode)
    path[...] = product
    lifted = tn_dot(product, node, exact_mode)
    tile_row = lax.broadcasted_iota(jnp.int32, (SUBLANES, LANES), 0)
    request = jnp.zeros((SUBLANES, LANES), f32)
    for k in range(wanted.shape[0]):
        request = jnp.where(tile_row == k, wanted[k].astype(f32), request)
    across = width // LANES
    for c in range(send.shape[0]):
        r, q = (c // across) * SUBLANES, (c % across) * LANES
        send[c, 0] = node[r : r + SUBLANES, q : q + LANES].astype(bf16)
        send[c, 1] = lifted[r : r + SUBLANES, q : q + LANES].astype(bf16)
        send[c, 2] = request.astype(bf16)


def near_kernel(use_before, use_after, rows_aug, vals_cols, before, after, out):
    leaves, leaf_rows, _ = rows_aug.shape
    width = out.shape[2]

    def part(rows, block):
        tile = jnp.exp(nt_dot(rows, block[:, width : width + LANES])).astype(bf16)
        return nn_dot(tile, block[:, 0:width])

    half = leaf_rows // 2
    for leaf in range(leaves):
        left = before[...] if leaf == 0 else vals_cols[leaf - 1]
        right = after[...] if leaf == leaves - 1 else vals_cols[leaf + 1]
        for piece in range(2):
            r = slice(piece * half, piece * half + half)
            rows = rows_aug[leaf, r, :]
            total = part(rows, vals_cols[leaf])
            total = total + use_before[leaf] * part(rows, left)
            total = total + use_after[leaf] * part(rows, right)
            out[leaf, r, :] = total


def root_kernel(received, root):
    total = received[0, 1].astype(f32)
    for j in range(1, received.shape[0]):
        total = total + received[j, 1].astype(f32)
    root[...] = total.astype(bf16)


def choose_kernel(top_list, received, roots, out):
    peers = received.shape[0]
    pairs = out.shape[1] - top_list.shape[1]
    nodes = [received[j, 0] for j in range(peers)]
    tops = [roots[top_list[0, k]] for k in range(top_list.shape[1])]
    for j in range(peers):
        asked = received[j, 2].astype(f32)
        for k in range(pairs):
            offset = jnp.broadcast_to(asked[k : k + 1, :], (SUBLANES, LANES))
            picked = jnp.zeros((SUBLANES, LANES), f32)
            for slot in range(2 * REACH + 1):
                source = j + slot - REACH
                if slot != REACH and 0 <= source < peers:
                    picked = jnp.where(offset == slot, nodes[source].astype(f32), picked)
            out[j, k] = picked.astype(bf16)
        for k, top in enumerate(tops):
            out[j, pairs + k] = top


def final_kernel(
    order,
    pair_count,
    received,
    pair_coupling,
    top_coupling,
    path,
    basis,
    transfer,
    near,
    out,
    held,
):
    leaves, leaf_rows, rank = basis.shape
    width = near.shape[2]
    across = width // LANES
    pairs = pair_coupling.shape[1]
    tops = top_coupling.shape[1]

    def source(k):
        bands = []
        for c in range(0, received.shape[0], across):
            parts = [received[c + q, k].astype(f32) for q in range(across)]
            bands.append(jnp.concatenate(parts, axis=1))
        return jnp.concatenate(bands, axis=0).astype(bf16)

    top_field = jnp.zeros((rank, width), f32)
    for k in range(tops):
        top_field = top_field + nn_dot(top_coupling[0, k], source(pairs + k))
    node_field = nn_dot(path[...], top_field, exact_mode)
    for k in range(pairs):
        term = nn_dot(pair_coupling[0, k], source(k))
        node_field = node_field + jnp.where(k < pair_count[0], term, 0.0)
    high, low = high_low(node_field)
    for leaf in range(leaves):
        field = (nn_dot(transfer[leaf], high) + nn_dot(transfer[leaf], low)).astype(bf16)
        far = nn_dot(basis[leaf], field)
        total = far + near[leaf]
        r = pl.ds(leaf * leaf_rows, leaf_rows)
        for q in range(across):
            held[r, q, :] = total[:, q * LANES : (q + 1) * LANES]

    def move(p):
        out[order[0, p]] = held[p]

    row_loop(leaves * leaf_rows, move)


def exchange(array, axis):
    return lax.all_to_all(array, axis, 0, 0, tiled=True)


def shifted(block, axis, distance):
    devices = range(lax.axis_size(axis))
    route = [(i - distance, i) for i in devices if i - distance in devices]
    return lax.ppermute(block, axis, route)


def call(kernel, args, specs, out_shapes, scratch=(), flops=0, moved=0):
    return pl.pallas_call(
        kernel,
        out_shape=out_shapes,
        in_specs=specs,
        out_specs=jax.tree.map(lambda _: VMEM_SPEC, out_shapes),
        scratch_shapes=list(scratch),
        compiler_params=pltpu.CompilerParams(vmem_limit_bytes=VMEM_LIMIT),
        cost_estimate=pl.CostEstimate(flops=flops, bytes_accessed=moved, transcendentals=0),
    )(*args)


def per_device(
    points,
    vectors,
    inv_length,
    order,
    leaf_basis,
    leaf_transfer,
    level_transfer,
    near_list,
    near_count,
    pair_list,
    pair_count,
    pair_coupling,
    top_list,
    top_coupling,
):
    sub_count = lax.axis_size("sub")
    levels_count = sub_count.bit_length() - 1
    sub_pos = lax.axis_index("sub")
    top_count = lax.axis_size("leaf")
    dev_pos = lax.axis_index("leaf") * sub_count + sub_pos
    leaf_count, leaf_rows, rank = leaf_basis.shape
    per_dev, features = points.shape
    width = vectors.shape[1] * vectors.shape[2]
    pairs = pair_list.shape[1]
    tops = top_list.shape[1]

    wanted = jnp.clip(pair_list[0] - dev_pos + REACH, 0, 2 * REACH)
    matrices = [
        lax.dynamic_slice_in_dim(
            level_transfer,
            2 * sub_count - 2 * (sub_count >> depth) + jnp.right_shift(sub_pos, depth),
            1,
            axis=1,
        )
        for depth in range(levels_count)
    ]
    vals_cols, rows_aug, send, path = call(
        gather_kernel,
        (
            order,
            wanted,
            vectors,
            points,
            inv_length[None],
            leaf_basis,
            leaf_transfer,
            *matrices,
        ),
        [SMEM_SPEC] * 2 + [VMEM_SPEC] * 10,
        (
            jax.ShapeDtypeStruct((leaf_count, leaf_rows, width + LANES), bf16),
            jax.ShapeDtypeStruct((leaf_count, leaf_rows, LANES), bf16),
            jax.ShapeDtypeStruct((sub_count, 3, SUBLANES, LANES), bf16),
            jax.ShapeDtypeStruct((rank, rank), f32),
        ),
        (
            pltpu.VMEM((per_dev, LANES), f32),
            pltpu.VMEM(vectors.shape, bf16),
            pltpu.VMEM((per_dev, LANES), f32),
        ),
        flops=1 << 29,
        moved=1 << 23,
    )

    before = shifted(vals_cols[leaf_count - 1], "sub", 1)
    after = shifted(vals_cols[0], "sub", -1)

    received = exchange(send, "sub")
    tile = jax.ShapeDtypeStruct((SUBLANES, LANES), bf16)
    root = call(root_kernel, (received,), [VMEM_SPEC], tile)
    roots = exchange(jnp.broadcast_to(root[None], (top_count, *root.shape)), "leaf")
    chosen = call(
        choose_kernel,
        (top_list, received, roots),
        [SMEM_SPEC, VMEM_SPEC, VMEM_SPEC],
        jax.ShapeDtypeStruct((sub_count, pairs + tops, SUBLANES, LANES), bf16),
    )
    sources = exchange(chosen, "sub")

    own = dev_pos * leaf_count + jnp.arange(leaf_count, dtype=jnp.int32)[:, None]
    used = jnp.arange(near_list.shape[1], dtype=jnp.int32)[None] < near_count[:, None]
    use_before = jnp.any(used & (near_list == own - 1), axis=1).astype(f32)
    use_after = jnp.any(used & (near_list == own + 1), axis=1).astype(f32)
    near = call(
        near_kernel,
        (use_before, use_after, rows_aug, vals_cols, before, after),
        [SMEM_SPEC] * 2 + [VMEM_SPEC] * 4,
        jax.ShapeDtypeStruct((leaf_count, leaf_rows, width), f32),
        flops=6 << 30,
        moved=1 << 23,
    )

    return call(
        final_kernel,
        (
            order,
            pair_count,
            sources,
            pair_coupling,
            top_coupling,
            path,
            leaf_basis,
            leaf_transfer,
            near,
        ),
        [SMEM_SPEC] * 2 + [VMEM_SPEC] * 7,
        jax.ShapeDtypeStruct(vectors.shape, f32),
        (pltpu.VMEM(vectors.shape, f32),),
        flops=1 << 29,
        moved=1 << 23,
    )


def solution(mesh):
    return jax.shard_map(
        per_device,
        mesh=mesh,
        in_specs=(
            P(("leaf", "sub"), None),
            P(("leaf", "sub"), None, None),
            P(),
            P(("leaf", "sub"), None),
            P(("leaf", "sub"), None, None),
            P(("leaf", "sub"), None, None),
            P("leaf", None, None, None),
            P(("leaf", "sub"), None),
            P(("leaf", "sub")),
            P(("leaf", "sub"), None),
            P(("leaf", "sub")),
            P(("leaf", "sub"), None, None, None),
            P("leaf", None),
            P("leaf", None, None, None),
        ),
        out_specs=P(("leaf", "sub"), None, None),
        check_vma=False,
    )
```

time: 344 us -> 97.4 us (0.28)
  the two profiles are of different devices: /device:TPU:102 before, /device:TPU:1 now
where the time goes in v1:
time: 97.4 us; the launch traced here: 96.9 us
  Pallas kernels  45.9 us (47%)
  starting transfers between devices  30.3 us (31%)
  local copies, waits for them, and re-layouts  9.19 us (9%)
  waiting for transfers between devices  8.38 us (9%)
  other arithmetic  2.37 us (2%)
    pallas_call x5, Pallas kernels, call(): pl.pallas_call(kernel, out_shape=out_shapes, in_specs=specs, out_specs=ja...  45.9 us
    all_to_all x3, starting transfers between devices, exchange(): return lax.all_to_all(array, axis, 0, 0, tiled=True)  25.8 us
    all_to_all x3, waiting for transfers between devices, exchange(): return lax.all_to_all(array, axis, 0, 0, tiled=True)  8.37 us
    unnamed x15, local copies, waits for them, and re-layouts  5.2 us
    ppermute x2, starting transfers between devices, shifted(): return lax.ppermute(block, axis, route)  4.45 us
  transfers between devices with their start and end apart: 5, of which 2 were waited for; matrix products, arithmetic and copies ran while one was open for 4% of the time, Pallas kernels for 17%

profile of v1, /device:TPU:1, one launch (start us, length us, event | category | flops | bytes accessed | tf_op | source)
XLA Modules:
  0.0 96.9 jit_solution(670846790469749006)
XLA Ops:
  0.0 2.3 %copy.15.points = bf16[4096,32]{1,0:T(8,128)(2,1)} copy(bf16[4096,32]{0,1:T(8,128)(2,1)} %param.14) | data formatting | bytes 524288 | tf_op args[0]
  2.3 1.2 %clamp_bitcast_fusion.wanted = s32[3]{0:T(128)} fusion(s32[1,3]{1,0:T(1,128)} %param.23, s32[]{:T(128)S(6)} %add.61), kind=kLoop, calls=%fused_computation.15 | loop fusion | flops 9 | bytes 28 | tf_op jit(solution)/shard_map/jit(clip)/min | solution.py:290
  3.4 1.5 %constant_dynamic-slice_fusion = (bf16[1,1,128,128]{3,2,1,0:T(8,128)(2,1)}, bf16[1,1,128,128]{3,2,1,0:T(8,128)(2,1)}, bf16[1,1,128,128]{3,2,1,0:T(8,128)(2,1)}, ...) fusion(bf16[1,62,128,128]{3,2,1,0:T(8,128)(2,1)} %param.20, s32[]{:T(128)S(6)} %select_n.19, s32[]{:T(128)S(6)} %select_n.17, ...), kind=kLoop, calls=%fused_computation.7 | loop fusion | bytes 327700 | tf_op jit(solution)/shard_map/dynamic_slice | solution.py:292
  5.0 0.0 copy-start.3
  5.0 0.0 copy-start.4
  5.0 16.1 %shard_map.136 = (bf16[8,512,384]{2,1,0:T(8,128)(2,1)}, bf16[8,512,128]{2,1,0:T(8,128)(2,1)}, bf16[32,3,8,128]{3,2,1,0:T(8,128)(2,1)}, f32[128,128]{1,0:T(8,128)}) custom-call(s32[1,4096]{1,0:T(1,128)} %order.3, s32[3]{0:T(128)} %clamp_bitcast_fusion.wanted, bf16[4096,2,128]{2,1,0:T(2,128)(2,1)} %vectors.1, bf16[4096,32]{1,0:T(8,128)(2,1)} %copy.15.points, ...), custom_call_target="tpu_custom_call" | custom-call | flops 536870912 | bytes 8388608 | tf_op jit(solution)/shard_map/pallas_call | solution.py:252
  21.0 11.9 %all-to-all-start = ((bf16[32,3,8,128]{3,2,1,0:T(8,128)(2,1)}), bf16[32,3,8,128]{3,2,1,0:T(8,128)(2,1)S(1)}, u32[]{:S(2)}, u32[]{:S(2)}) async-start(bf16[32,3,8,128]{3,2,1,0:T(8,128)(2,1)} %get-tuple-element.9), calls=%async_computation | async-start | bytes 393216 | tf_op jit(solution)/shard_map/all_to_all | solution.py:242
  32.9 1.2 %slice_bitcast_fusion = (bf16[512,384]{1,0:T(8,128)(2,1)S(1)}, bf16[512,384]{1,0:T(8,128)(2,1)S(1)}) fusion(bf16[8,512,384]{2,1,0:T(8,128)(2,1)} %get-tuple-element.12.vals_cols), kind=kLoop, calls=%fused_computation | loop fusion | bytes 1572864 | tf_op jit(solution)/shard_map/squeeze | solution.py:329
  34.1 3.2 %collective-permute-start = (bf16[512,384]{1,0:T(8,128)(2,1)S(1)}, bf16[512,384]{1,0:T(8,128)(2,1)S(1)}, u32[]{:S(2)}, u32[]{:S(2)}) collective-permute-start(bf16[512,384]{1,0:T(8,128)(2,1)S(1)} %get-tuple-element.16), channel_id=1, source_target_pairs={{0,1},{1,2},{2,3},{3,4},{4,5},{5,6},{6,7},{7,8},{8,9},{9,10},{10,1... | collective-permute-start | bytes 1179656 | tf_op jit(solution)/shard_map/ppermute | solution.py:248
  37.3 1.3 %collective-permute-start.1 = (bf16[512,384]{1,0:T(8,128)(2,1)S(1)}, bf16[512,384]{1,0:T(8,128)(2,1)S(1)}, u32[]{:S(2)}, u32[]{:S(2)}) collective-permute-start(bf16[512,384]{1,0:T(8,128)(2,1)S(1)} %get-tuple-element.15), channel_id=1, source_target_pairs={{1,0},{2,1},{3,2},{4,3},{5,4},{6,5},{7,6},{8,7},{9,8},{10,9},{11,1... | collective-permute-start | bytes 1179656 | tf_op jit(solution)/shard_map/ppermute | solution.py:248
  38.6 3.7 %all-to-all-done.received = bf16[32,3,8,128]{3,2,1,0:T(8,128)(2,1)S(1)} async-done(((bf16[32,3,8,128]{3,2,1,0:T(8,128)(2,1)}), bf16[32,3,8,128]{3,2,1,0:T(8,128)(2,1)S(1)}, u32[]{:S(2)}, u32[]{:S(2)}) %all-to-all-start) | async-done | bytes 196640 | tf_op jit(solution)/shard_map/all_to_all | solution.py:242
  42.3 0.0 copy-start
  42.3 0.7 copy-done
  43.0 1.6 %shard_map.137 = bf16[8,128]{1,0:T(8,128)(2,1)} custom-call(bf16[32,3,8,128]{3,2,1,0:T(8,128)(2,1)} %copy-done), custom_call_target="tpu_custom_call" | custom-call | tf_op jit(solution)/shard_map/pallas_call | solution.py:252
  44.5 1.3 %broadcast_in_dim.5 = bf16[8,8,128]{2,1,0:T(8,128)(2,1)} broadcast(bf16[8,128]{1,0:T(8,128)(2,1)} %shard_map.137), dimensions={1,2} | broadcast | bytes 18432 | tf_op jit(solution)/shard_map/broadcast_in_dim | solution.py:334
  45.8 7.3 %all-to-all-start.1 = ((bf16[8,8,128]{2,1,0:T(8,128)(2,1)}), bf16[8,8,128]{2,1,0:T(8,128)(2,1)S(1)}, u32[]{:S(2)}, u32[]{:S(2)}) async-start(bf16[8,8,128]{2,1,0:T(8,128)(2,1)} %broadcast_in_dim.5), calls=%async_computation.1 | async-start | bytes 32768 | tf_op jit(solution)/shard_map/all_to_all | solution.py:242
  53.2 4.6 %all-to-all-done.1.roots = bf16[8,8,128]{2,1,0:T(8,128)(2,1)S(1)} async-done(((bf16[8,8,128]{2,1,0:T(8,128)(2,1)}), bf16[8,8,128]{2,1,0:T(8,128)(2,1)S(1)}, u32[]{:S(2)}, u32[]{:S(2)}) %all-to-all-start.1) | async-done | bytes 16416 | tf_op jit(solution)/shard_map/all_to_all | solution.py:242
  57.8 0.0 copy-start.2
  57.8 0.6 copy-done.2
  58.4 1.9 %shard_map.138 = bf16[32,5,8,128]{3,2,1,0:T(8,128)(2,1)} custom-call(s32[1,2]{1,0:T(1,128)} %top_list.1, bf16[32,3,8,128]{3,2,1,0:T(8,128)(2,1)} %copy-done, bf16[8,8,128]{2,1,0:T(8,128)(2,1)} %copy-done.2), custom_call_target="tpu_custom_call" | custom-call | tf_op jit(solution)/shard_map/pallas_call | solution.py:252
  60.3 6.6 %all-to-all-start.2 = ((bf16[32,5,8,128]{3,2,1,0:T(8,128)(2,1)}), bf16[32,5,8,128]{3,2,1,0:T(8,128)(2,1)S(1)}, u32[]{:S(2)}, u32[]{:S(2)}) async-start(bf16[32,5,8,128]{3,2,1,0:T(8,128)(2,1)} %shard_map.138), calls=%async_computation.2 | async-start | bytes 655360 | tf_op jit(solution)/shard_map/all_to_all | solution.py:242
  67.0 0.0 copy-done.3
  67.0 0.0 copy-done.4
  67.0 0.6 convert_element_type.6.use_before
  67.6 0.6 convert_element_type.7.use_after
  68.9 0.0 collective-permute-done.before
  68.9 0.0 copy-start.5
  68.9 0.0 collective-permute-done.1.after
  68.9 0.0 copy-start.6
  68.9 0.7 copy-done.5
  69.6 0.2 copy-done.6
  69.8 13.1 %shard_map.139.near = f32[8,512,256]{2,1,0:T(8,128)} custom-call(f32[8]{0:T(128)} %convert_element_type.6.use_before, f32[8]{0:T(128)} %convert_element_type.7.use_after, bf16[8,512,128]{2,1,0:T(8,128)(2,1)} %get-tuple-element.11.rows_aug, bf16[8,512,384]{2,1,0:T(8,128)(2,1)} %get-tuple-element.12.vals_cols, bf16[512,384]{1,0:T(8,128)(2,1)} %copy-done.5, ...), custom_call_target="tpu_custom_call" | custom-call | flops 6442450944 | bytes 8388608 | tf_op jit(solution)/shard_map/pallas_call | solution.py:252
  82.9 0.0 all-to-all-done.2.received
  82.9 0.0 copy-start.1
  82.9 0.7 copy-done.1
  83.7 13.2 %shard_map.140 = f32[4096,2,128]{2,1,0:T(2,128)} custom-call(s32[1,4096]{1,0:T(1,128)} %order.3, s32[1]{0:T(128)S(6)} %copy.16.pair_count, bf16[32,5,8,128]{3,2,1,0:T(8,128)(2,1)} %copy-done.1, bf16[1,3,128,128]{3,2,1,0:T(8,128)(2,1)} %pair_coupling.1, bf16[1,2,128,128]{3,2,1,0:T(8,128)(2,1)} %top_coupling.1, f32[128,128]{1,0:T(8,128)} %get-tuple-element.10.path, ...), custom_call_target="tpu_custom_call" | custom-call | flops 536870912 | bytes 8388608 | tf_op jit(solution)/shard_map/pallas_call | solution.py:252
  (2 shorter events, 0.0 us)
Async XLA Ops:
  5.0 62.0 %copy-start.3 = (s32[8,3]{0,1:T(4,128)S(1)}, s32[8,3]{0,1:T(4,128)}, u32[]{:S(2)}) copy-start(s32[8,3]{0,1:T(4,128)} %param.21) | copy-start | bytes 292
  5.0 62.0 %copy-start.4 = (s32[8]{0:T(128)S(1)}, s32[8]{0:T(128)}, u32[]{:S(2)}) copy-start(s32[8]{0:T(128)} %param.22) | copy-start | bytes 100
  21.0 21.3 %all-to-all-start = ((bf16[32,3,8,128]{3,2,1,0:T(8,128)(2,1)}), bf16[32,3,8,128]{3,2,1,0:T(8,128)(2,1)S(1)}, u32[]{:S(2)}, u32[]{:S(2)}) async-start(bf16[32,3,8,128]{3,2,1,0:T(8,128)(2,1)} %get-tuple-element.9), calls=%async_computation | async-start | bytes 393216 | tf_op jit(solution)/shard_map/all_to_all | solution.py:242
  34.1 34.7 %collective-permute-start = (bf16[512,384]{1,0:T(8,128)(2,1)S(1)}, bf16[512,384]{1,0:T(8,128)(2,1)S(1)}, u32[]{:S(2)}, u32[]{:S(2)}) collective-permute-start(bf16[512,384]{1,0:T(8,128)(2,1)S(1)} %get-tuple-element.16), channel_id=1, source_target_pairs={{0,1},{1,2},{2,3},{3,4},{4,5},{5,6},{6,7},{7,8},{8,9},{9,10},{10,1... | collective-permute-start | bytes 1179656 | tf_op jit(solution)/shard_map/ppermute | solution.py:248
  37.3 31.6 %collective-permute-start.1 = (bf16[512,384]{1,0:T(8,128)(2,1)S(1)}, bf16[512,384]{1,0:T(8,128)(2,1)S(1)}, u32[]{:S(2)}, u32[]{:S(2)}) collective-permute-start(bf16[512,384]{1,0:T(8,128)(2,1)S(1)} %get-tuple-element.15), channel_id=1, source_target_pairs={{1,0},{2,1},{3,2},{4,3},{5,4},{6,5},{7,6},{8,7},{9,8},{10,9},{11,1... | collective-permute-start | bytes 1179656 | tf_op jit(solution)/shard_map/ppermute | solution.py:248
  42.3 0.7 copy-start
  45.8 12.0 %all-to-all-start.1 = ((bf16[8,8,128]{2,1,0:T(8,128)(2,1)}), bf16[8,8,128]{2,1,0:T(8,128)(2,1)S(1)}, u32[]{:S(2)}, u32[]{:S(2)}) async-start(bf16[8,8,128]{2,1,0:T(8,128)(2,1)} %broadcast_in_dim.5), calls=%async_computation.1 | async-start | bytes 32768 | tf_op jit(solution)/shard_map/all_to_all | solution.py:242
  57.8 0.6 copy-start.2
  60.3 22.6 %all-to-all-start.2 = ((bf16[32,5,8,128]{3,2,1,0:T(8,128)(2,1)}), bf16[32,5,8,128]{3,2,1,0:T(8,128)(2,1)S(1)}, u32[]{:S(2)}, u32[]{:S(2)}) async-start(bf16[32,5,8,128]{3,2,1,0:T(8,128)(2,1)} %shard_map.138), calls=%async_computation.2 | async-start | bytes 655360 | tf_op jit(solution)/shard_map/all_to_all | solution.py:242
  68.9 0.8 copy-start.5
  68.9 0.9 copy-start.6
  82.9 0.7 copy-start.1

commit v2 on v1

v2 whole, which is shorter than its diff:
```python
import functools

import jax
import jax.numpy as jnp
from jax import lax
from jax.experimental import pallas as pl
from jax.experimental.pallas import tpu as pltpu
from jax.sharding import PartitionSpec as P

REACH = 4
LANES = 128
SUBLANES = 8
VMEM_LIMIT = 60 << 20
SMALL_LIMIT = 4 << 20
FINAL_LIMIT = 40 << 20
NEAR_LIMIT = 40 << 20
UNROLL = 64
BLOCK = 512
NEAR_GROUPS = ((1, 2, 3), (4, 5, 6, 0, 7))

bf16 = jnp.bfloat16
f32 = jnp.float32
exact_mode = lax.Precision.HIGHEST

SMEM_SPEC = pl.BlockSpec(memory_space=pltpu.SMEM)
VMEM_SPEC = pl.BlockSpec(memory_space=pltpu.VMEM)
ANY_SPEC = pl.BlockSpec(memory_space=pl.ANY)


def tn_dot(a, b, precision=None):
    return lax.dot_general(
        a, b, (((0,), (0,)), ((), ())), preferred_element_type=f32, precision=precision
    )


def nt_dot(a, b):
    return lax.dot_general(a, b, (((1,), (1,)), ((), ())), preferred_element_type=f32)


def nn_dot(a, b, precision=None):
    return lax.dot_general(
        a, b, (((1,), (0,)), ((), ())), preferred_element_type=f32, precision=precision
    )


def high_low(x):
    high = x.astype(bf16)
    return high, (x - high.astype(f32)).astype(bf16)


def row_loop(rows, step):
    def several(i, carry):
        for k in range(UNROLL):
            step(i * UNROLL + k)
        return carry

    lax.fori_loop(0, rows // UNROLL, several, 0)


def chunk_loop(rows, size, step):
    def one(i, carry):
        step(pl.ds(pl.multiple_of(i * size, size), size), i)
        return carry

    lax.fori_loop(0, rows // size, one, 0)


def gather_kernel(
    order,
    position,
    pair_list,
    vectors_hbm,
    points_hbm,
    inv_length,
    basis_hbm,
    transfer_hbm,
    levels_hbm,
    vals_cols_hbm,
    rows_aug_hbm,
    first_hbm,
    last_hbm,
    send,
    path,
    vals_cols,
    rows_aug,
    vectors,
    points,
    basis,
    transfer,
    mats,
    table,
    held_vals,
    held_points,
    sems,
    out_sems,
):
    leaves, leaf_rows, rank = basis.shape
    features, per_dev = points.shape
    width = vectors.shape[1] * vectors.shape[2]
    levels = mats.shape[0]
    sub_count = 1 << levels
    dev_pos, sub_pos = position[0], position[1]

    copies = [
        pltpu.make_async_copy(points_hbm, points, sems.at[0]),
        pltpu.make_async_copy(vectors_hbm, vectors, sems.at[1]),
        pltpu.make_async_copy(basis_hbm, basis, sems.at[2]),
        pltpu.make_async_copy(transfer_hbm, transfer, sems.at[3]),
    ]
    for depth in range(levels):
        node = 2 * sub_count - 2 * (sub_count >> depth) + jnp.right_shift(sub_pos, depth)
        copies.append(
            pltpu.make_async_copy(levels_hbm.at[0, node], mats.at[depth], sems.at[4 + depth])
        )
    for copy in copies:
        copy.start()

    lane = lax.broadcasted_iota(jnp.int32, (1, LANES), 1)
    piece = lane - features

    spare = jnp.zeros((SUBLANES, BLOCK), f32)
    row = lax.broadcasted_iota(jnp.int32, (SUBLANES, BLOCK), 0)
    here = lax.broadcasted_iota(jnp.int32, (features, features), 0)
    there = lax.broadcasted_iota(jnp.int32, (features, features), 1)
    scale = jnp.sum(jnp.where(here == there, inv_length[...], 0.0), axis=1, keepdims=True)

    def augment(r, i):
        x = (points[:, r].astype(f32) * scale).astype(bf16).astype(f32)
        half = -0.5 * jnp.sum(x * x, axis=0, keepdims=True)
        h1 = half.astype(bf16).astype(f32)
        h2 = (half - h1).astype(bf16).astype(f32)
        h3 = half - h1 - h2
        extra = jnp.where(row % 3 == 0, h1, jnp.where(row % 3 == 1, h2, h3))
        extra = jnp.where(row < 6, extra, 0.0)
        pads = [spare] * ((LANES - features) // SUBLANES - 1)
        table[r, :] = jnp.concatenate([x, extra, *pads], axis=0).T

    copies[0].wait()
    chunk_loop(per_dev, BLOCK, augment)

    def move(p):
        source = order[0, p]
        held_vals[p] = vectors[source]
        held_points[pl.ds(p, 1), :] = table[pl.ds(source, 1), :]

    copies[1].wait()
    row_loop(per_dev, move)

    for copy in copies[2:]:
        copy.wait()
    ones_left = (piece >= 0) & (piece < 3)
    ones_right = (piece >= 3) & (piece < 6)
    stores = []
    node = jnp.zeros((rank, width), f32)
    for leaf in range(leaves):
        base = leaf * leaf_rows
        vals = held_vals[base : base + leaf_rows].reshape(leaf_rows, width)
        got = held_points[base : base + leaf_rows, :]
        cols = jnp.where(ones_left, 1.0, got).astype(bf16)
        vals_cols[leaf, :, 0:width] = vals
        vals_cols[leaf, :, width : width + LANES] = cols
        rows_aug[leaf] = jnp.where(ones_right, 1.0, got).astype(bf16)
        places = [
            (vals_cols.at[leaf], vals_cols_hbm.at[leaf], 2 * leaf),
            (rows_aug.at[leaf], rows_aug_hbm.at[leaf], 2 * leaf + 1),
        ]
        if leaf == 0:
            places.append((vals_cols.at[leaf], first_hbm, 2 * leaves))
        if leaf == leaves - 1:
            places.append((vals_cols.at[leaf], last_hbm, 2 * leaves + 1))
        for source, target, slot in places:
            stores.append(pltpu.make_async_copy(source, target, out_sems.at[slot]))
            stores[-1].start()
        coef = tn_dot(basis[leaf], vals)
        high, low = high_low(coef)
        node = node + tn_dot(transfer[leaf], high) + tn_dot(transfer[leaf], low)

    product = mats[0].astype(f32)
    for depth in range(1, levels):
        product = nn_dot(product, mats[depth].astype(f32), exact_mode)
    path[...] = product
    lifted = tn_dot(product, node, exact_mode)
    tile_row = lax.broadcasted_iota(jnp.int32, (SUBLANES, LANES), 0)
    request = jnp.zeros((SUBLANES, LANES), f32)
    for k in range(pair_list.shape[1]):
        offset = jnp.clip(pair_list[0, k] - dev_pos + REACH, 0, 2 * REACH)
        request = jnp.where(tile_row == k, offset.astype(f32), request)
    across = width // LANES
    for c in range(send.shape[0]):
        r, q = (c // across) * SUBLANES, (c % across) * LANES
        send[c, 0] = node[r : r + SUBLANES, q : q + LANES].astype(bf16)
        send[c, 1] = lifted[r : r + SUBLANES, q : q + LANES].astype(bf16)
        send[c, 2] = request.astype(bf16)
    for copy in stores:
        copy.wait()


def near_kernel(members, position, near_list, near_count, rows_hbm, cols_hbm, *rest):
    *edges, out_hbm, rows_aug, vals_cols, ends, out, in_sems, out_sems = rest
    leaves, _, _ = rows_aug.shape
    width = out.shape[2]

    loads = {}

    def want(key, source, target):
        if key not in loads:
            copy = pltpu.make_async_copy(source, target, in_sems.at[len(loads)])
            copy.start()
            loads[key] = [copy, False]

    def block(index):
        if 0 <= index < leaves:
            return ("cols", index), cols_hbm.at[index], vals_cols.at[index]
        side = 0 if index < 0 else 1
        return ("edge", side), edges[side], ends.at[side]

    for leaf in members:
        want(("rows", leaf), rows_hbm.at[leaf], rows_aug.at[leaf])
        for index in (leaf, leaf - 1, leaf + 1):
            want(*block(index))

    def ready(key):
        entry = loads[key]
        if not entry[1]:
            entry[0].wait()
            entry[1] = True

    def flag(leaf, neighbour):
        own = position[0] * leaves + leaf
        found = jnp.int32(0)
        for k in range(near_list.shape[0]):
            hit = (k < near_count[leaf]) & (near_list[k, leaf] == own + neighbour)
            found = found | hit.astype(jnp.int32)
        return found.astype(f32)

    def part(rows, cols):
        tile = jnp.exp(nt_dot(rows, cols[:, width : width + LANES])).astype(bf16)
        return nn_dot(tile, cols[:, 0:width])

    stores = []
    for slot, leaf in enumerate(members):
        ready(("rows", leaf))
        for index in (leaf, leaf - 1, leaf + 1):
            ready(block(index)[0])
        left, right = block(leaf - 1)[2], block(leaf + 1)[2]
        use_left, use_right = flag(leaf, -1), flag(leaf, 1)
        rows = rows_aug[leaf]
        total = part(rows, vals_cols[leaf])
        total = total + use_left * part(rows, left[...])
        total = total + use_right * part(rows, right[...])
        out[slot] = total
        stores.append(pltpu.make_async_copy(out.at[slot], out_hbm.at[slot], out_sems.at[slot]))
        stores[-1].start()
    for copy in stores:
        copy.wait()


def root_kernel(received, roots):
    total = received[0, 1].astype(f32)
    for j in range(1, received.shape[0]):
        total = total + received[j, 1].astype(f32)
    for s in range(roots.shape[0]):
        roots[s] = total.astype(bf16)


def choose_kernel(top_list, received, roots, out):
    peers = received.shape[0]
    pairs = out.shape[1] - top_list.shape[1]
    nodes = [received[j, 0] for j in range(peers)]
    tops = [roots[top_list[0, k]] for k in range(top_list.shape[1])]
    for j in range(peers):
        asked = received[j, 2].astype(f32)
        for k in range(pairs):
            offset = jnp.broadcast_to(asked[k : k + 1, :], (SUBLANES, LANES))
            picked = jnp.zeros((SUBLANES, LANES), f32)
            for slot in range(2 * REACH + 1):
                source = j + slot - REACH
                if slot != REACH and 0 <= source < peers:
                    picked = jnp.where(offset == slot, nodes[source].astype(f32), picked)
            out[j, k] = picked.astype(bf16)
        for k, top in enumerate(tops):
            out[j, pairs + k] = top


def final_kernel(
    order,
    pair_count,
    received,
    pair_hbm,
    top_hbm,
    path_hbm,
    basis_hbm,
    transfer_hbm,
    *rest,
):
    *nears_hbm, out, held, near, pair_coupling, top_coupling, path, basis, transfer, sems = rest
    leaves, leaf_rows, rank = basis.shape
    width = near.shape[2]
    across = width // LANES
    pairs = pair_coupling.shape[1]
    tops = top_coupling.shape[1]

    def load(source, target, slot):
        copy = pltpu.make_async_copy(source, target, sems.at[slot])
        copy.start()
        return copy

    small = [
        load(top_hbm, top_coupling, 0),
        load(pair_hbm, pair_coupling, 1),
        load(transfer_hbm, transfer, 2),
        load(basis_hbm, basis, 3),
        load(path_hbm, path, 4),
    ]
    large = {}
    slots = [(group, i, leaf) for group, m in enumerate(NEAR_GROUPS) for i, leaf in enumerate(m)]
    for group, i, leaf in sorted(slots, key=lambda entry: entry[2]):
        large[leaf] = load(nears_hbm[group].at[i], near.at[leaf], 5 + leaf)

    def source(k):
        bands = []
        for c in range(0, received.shape[0], across):
            parts = [received[c + q, k].astype(f32) for q in range(across)]
            bands.append(jnp.concatenate(parts, axis=1))
        return jnp.concatenate(bands, axis=0).astype(bf16)

    small[0].wait()
    small[1].wait()
    top_field = jnp.zeros((rank, width), f32)
    for k in range(tops):
        top_field = top_field + nn_dot(top_coupling[0, k], source(pairs + k))
    small[4].wait()
    node_field = nn_dot(path[...], top_field, exact_mode)
    for k in range(pairs):
        term = nn_dot(pair_coupling[0, k], source(k))
        node_field = node_field + jnp.where(k < pair_count[0], term, 0.0)
    high, low = high_low(node_field)
    small[2].wait()
    small[3].wait()
    for leaf in range(leaves):
        field = (nn_dot(transfer[leaf], high) + nn_dot(transfer[leaf], low)).astype(bf16)
        far = nn_dot(basis[leaf], field)
        large[leaf].wait()
        total = far + near[leaf]
        r = pl.ds(leaf * leaf_rows, leaf_rows)
        for q in range(across):
            held[r, q, :] = total[:, q * LANES : (q + 1) * LANES]

    def move(p):
        out[order[0, p]] = held[p]

    row_loop(leaves * leaf_rows, move)


def exchange(array, axis):
    return lax.all_to_all(array, axis, 0, 0, tiled=True)


def shifted(block, axis, distance):
    devices = range(lax.axis_size(axis))
    route = [(i - distance, i) for i in devices if i - distance in devices]
    return lax.ppermute(block, axis, route)


def call(kernel, args, specs, outs, scratch=(), out_specs=None, limit=VMEM_LIMIT, flops=0):
    return pl.pallas_call(
        kernel,
        out_shape=outs,
        in_specs=specs,
        out_specs=jax.tree.map(lambda _: VMEM_SPEC, outs) if out_specs is None else out_specs,
        scratch_shapes=list(scratch),
        compiler_params=pltpu.CompilerParams(vmem_limit_bytes=limit),
        cost_estimate=pl.CostEstimate(
            flops=flops, bytes_accessed=flops // 512, transcendentals=0
        ),
    )(*args)


def off_chip(array):
    return pltpu.with_memory_space_constraint(array, pltpu.HBM)


def per_device(
    points,
    vectors,
    inv_length,
    order,
    leaf_basis,
    leaf_transfer,
    level_transfer,
    near_list,
    near_count,
    pair_list,
    pair_count,
    pair_coupling,
    top_list,
    top_coupling,
):
    sub_count = lax.axis_size("sub")
    levels_count = sub_count.bit_length() - 1
    sub_pos = lax.axis_index("sub")
    top_count = lax.axis_size("leaf")
    dev_pos = lax.axis_index("leaf") * sub_count + sub_pos
    leaf_count, leaf_rows, rank = leaf_basis.shape
    per_dev, features = points.shape
    width = vectors.shape[1] * vectors.shape[2]
    pairs = pair_list.shape[1]
    tops = top_list.shape[1]
    position = jnp.stack([dev_pos, sub_pos]).astype(jnp.int32)
    edge = jax.ShapeDtypeStruct((leaf_rows, width + LANES), bf16)

    ext_shape = (leaf_count, leaf_rows, width + LANES)
    aug_shape = (leaf_count, leaf_rows, LANES)
    vals_cols, rows_aug, first_leaf, last_leaf, send, path = call(
        gather_kernel,
        (
            order,
            position,
            pair_list,
            off_chip(vectors),
            off_chip(points.T),
            inv_length[None],
            off_chip(leaf_basis),
            off_chip(leaf_transfer),
            off_chip(level_transfer),
        ),
        [SMEM_SPEC] * 3 + [ANY_SPEC] * 2 + [VMEM_SPEC] + [ANY_SPEC] * 3,
        (
            jax.ShapeDtypeStruct(ext_shape, bf16),
            jax.ShapeDtypeStruct(aug_shape, bf16),
            edge,
            edge,
            jax.ShapeDtypeStruct((sub_count, 3, SUBLANES, LANES), bf16),
            jax.ShapeDtypeStruct((rank, rank), f32),
        ),
        (
            pltpu.VMEM(ext_shape, bf16),
            pltpu.VMEM(aug_shape, bf16),
            pltpu.VMEM(vectors.shape, bf16),
            pltpu.VMEM((features, per_dev), bf16),
            pltpu.VMEM(leaf_basis.shape, bf16),
            pltpu.VMEM(leaf_transfer.shape, bf16),
            pltpu.VMEM((levels_count, rank, rank), bf16),
            pltpu.VMEM((per_dev, LANES), f32),
            pltpu.VMEM(vectors.shape, bf16),
            pltpu.VMEM((per_dev, LANES), f32),
            pltpu.SemaphoreType.DMA((4 + levels_count,)),
            pltpu.SemaphoreType.DMA((2 * leaf_count + 2,)),
        ),
        (ANY_SPEC,) * 4 + (VMEM_SPEC,) * 2,
        flops=1 << 29,
    )

    before = shifted(last_leaf, "sub", 1)
    after = shifted(first_leaf, "sub", -1)

    received = exchange(send, "sub")
    tile = (SUBLANES, LANES)
    own_root = call(
        root_kernel,
        (received,),
        [VMEM_SPEC],
        jax.ShapeDtypeStruct((top_count, *tile), bf16),
        limit=SMALL_LIMIT,
    )
    roots = exchange(own_root, "leaf")
    chosen = call(
        choose_kernel,
        (top_list, received, roots),
        [SMEM_SPEC, VMEM_SPEC, VMEM_SPEC],
        jax.ShapeDtypeStruct((sub_count, pairs + tops, *tile), bf16),
        limit=SMALL_LIMIT,
    )
    sources = exchange(chosen, "sub")

    nears = []
    for members in NEAR_GROUPS:
        needs_edges = 0 in members or leaf_count - 1 in members
        edges = (before, after) if needs_edges else ()
        near_shape = (len(members), leaf_rows, width)
        near = call(
            functools.partial(near_kernel, members),
            (
                off_chip(position),
                near_list.T,
                off_chip(near_count),
                off_chip(rows_aug),
                off_chip(vals_cols),
                *edges,
            ),
            [SMEM_SPEC] * 3 + [ANY_SPEC] * (2 + len(edges)),
            pltpu.HBM(near_shape, f32),
            (
                pltpu.VMEM(aug_shape, bf16),
                pltpu.VMEM(ext_shape, bf16),
                pltpu.VMEM((2, *ext_shape[1:]), bf16),
                pltpu.VMEM(near_shape, f32),
                pltpu.SemaphoreType.DMA((2 * leaf_count + 2,)),
                pltpu.SemaphoreType.DMA((len(members),)),
            ),
            ANY_SPEC,
            limit=NEAR_LIMIT,
            flops=3 << 30,
        )
        nears.append(near)

    return call(
        final_kernel,
        (
            off_chip(order),
            pair_count,
            sources,
            off_chip(pair_coupling),
            off_chip(top_coupling),
            off_chip(path),
            off_chip(leaf_basis),
            off_chip(leaf_transfer),
            *[off_chip(near) for near in nears],
        ),
        [SMEM_SPEC] * 2 + [VMEM_SPEC] + [ANY_SPEC] * (5 + len(nears)),
        jax.ShapeDtypeStruct(vectors.shape, f32),
        (
            pltpu.VMEM(vectors.shape, f32),
            pltpu.VMEM((leaf_count, leaf_rows, width), f32),
            pltpu.VMEM(pair_coupling.shape, bf16),
            pltpu.VMEM(top_coupling.shape, bf16),
            pltpu.VMEM((rank, rank), f32),
            pltpu.VMEM(leaf_basis.shape, bf16),
            pltpu.VMEM(leaf_transfer.shape, bf16),
            pltpu.SemaphoreType.DMA((5 + leaf_count,)),
        ),
        limit=FINAL_LIMIT,
        flops=1 << 29,
    )


def solution(mesh):
    return jax.shard_map(
        per_device,
        mesh=mesh,
        in_specs=(
            P(("leaf", "sub"), None),
            P(("leaf", "sub"), None, None),
            P(),
            P(("leaf", "sub"), None),
            P(("leaf", "sub"), None, None),
            P(("leaf", "sub"), None, None),
            P("leaf", None, None, None),
            P(("leaf", "sub"), None),
            P(("leaf", "sub")),
            P(("leaf", "sub"), None),
            P(("leaf", "sub")),
            P(("leaf", "sub"), None, None, None),
            P("leaf", None),
            P("leaf", None, None, None),
        ),
        out_specs=P(("leaf", "sub"), None, None),
        check_vma=False,
    )
```

time: 97.4 us -> 84.6 us (0.87)
  blocking collectives: 0 us -> 12.2 us
  local copies, waits for them, and re-layouts: 9.19 us -> 0.01 us
  starting transfers between devices: 30.3 us -> 21.2 us
  waiting for transfers between devices: 8.38 us -> 4.93 us
  other arithmetic: 2.37 us -> 0.59 us
  Pallas kernels: 45.9 us -> 44.2 us
    all_to_all x0 -> x1, blocking collectives: none -> 12.2 us  [exchange(): return lax.all_to_all(array, axis, 0, 0, tiled=True)]
    all_to_all x3 -> x2, starting transfers between devices: 25.8 us -> 16.7 us  [exchange(): return lax.all_to_all(array, axis, 0, 0, tiled=True)]
    unnamed x15 -> x4, local copies, waits for them, and re-layouts: 5.2 us -> 0.01 us
    all_to_all x3 -> x2, waiting for transfers between devices: 8.37 us -> 4.93 us  [exchange(): return lax.all_to_all(array, axis, 0, 0, tiled=True)]
    pallas_call x5 -> x6, Pallas kernels: 45.9 us -> 44.2 us  [call(): pl.pallas_call(kernel, out_shape=outs, in_specs=specs, out_specs=jax.tree...]
    dynamic_slice x1 -> x0, local copies, waits for them, and re-layouts: 1.51 us -> none  [per_device(): lax.dynamic_slice_in_dim(level_transfer, 2 * sub_count - 2 * (sub_count >...]
    broadcast_in_dim x1 -> x0, local copies, waits for them, and re-layouts: 1.28 us -> none  [per_device(): jnp.broadcast_to(root[None], (top_count, *root.shape))]
    squeeze x1 -> x0, local copies, waits for them, and re-layouts: 1.2 us -> none  [per_device(): after = shifted(vals_cols[0], 'sub', -1)]
  transfers between devices with their start and end apart: 5 -> 4, of which waited for: 2 -> 1; matrix products, arithmetic and copies ran while one was open for 4% -> 0% of each run, Pallas kernels for 17% -> 20%
where the time goes in v2:
time: 84.6 us; the launch traced here: 84 us
  Pallas kernels  44.2 us (52%)
  starting transfers between devices  21.2 us (25%)
  blocking collectives  12.2 us (14%)
  waiting for transfers between devices  4.93 us (6%)
  between operations  0.9 us (1%)
    pallas_call x6, Pallas kernels, call(): pl.pallas_call(kernel, out_shape=outs, in_specs=specs, out_specs=jax.tree...  44.2 us
    all_to_all x2, starting transfers between devices, exchange(): return lax.all_to_all(array, axis, 0, 0, tiled=True)  16.7 us
    all_to_all x1, blocking collectives, exchange(): return lax.all_to_all(array, axis, 0, 0, tiled=True)  12.2 us
    all_to_all x2, waiting for transfers between devices, exchange(): return lax.all_to_all(array, axis, 0, 0, tiled=True)  4.93 us
    ppermute x2, starting transfers between devices, shifted(): return lax.ppermute(block, axis, route)  4.45 us
  transfers between devices with their start and end apart: 4, of which 1 were waited for; matrix products, arithmetic and copies ran while one was open for 0% of the time, Pallas kernels for 20%

profile of v2, /device:TPU:1, one launch (start us, length us, event | category | flops | bytes accessed | tf_op | source)
XLA Modules:
  0.0 84.0 jit_solution(14250526784285019686)
XLA Ops:
  0.0 0.6 pad_add_fusion.position
  0.6 0.0 copy-start
  0.6 0.0 copy-start.1
  0.6 14.5 %shard_map.136 = (bf16[8,512,384]{2,1,0:T(8,128)(2,1)}, bf16[8,512,128]{2,1,0:T(8,128)(2,1)}, bf16[512,384]{1,0:T(8,128)(2,1)}, bf16[512,384]{1,0:T(8,128)(2,1)}...) custom-call(s32[1,4096]{1,0:T(1,128)} %order.3, s32[2]{0:T(128)} %pad_add_fusion.position, s32[1,3]{1,0:T(1,128)} %pair_list.1, ...), custom_call_target="tpu_custom_call" | custom-call | flops 536870912 | bytes 1048576 | tf_op jit(solution)/shard_map/pallas_call | solution.py:366
  15.1 11.9 %all-to-all-start = ((bf16[32,3,8,128]{3,2,1,0:T(8,128)(2,1)}), bf16[32,3,8,128]{3,2,1,0:T(8,128)(2,1)S(1)}, u32[]{:S(2)}, u32[]{:S(2)}) async-start(bf16[32,3,8,128]{3,2,1,0:T(8,128)(2,1)} %get-tuple-element.11), calls=%async_computation | async-start | bytes 393216 | tf_op jit(solution)/shard_map/all_to_all | solution.py:356
  26.9 3.2 %collective-permute-start = (bf16[512,384]{1,0:T(8,128)(2,1)}, bf16[512,384]{1,0:T(8,128)(2,1)S(1)}, u32[]{:S(2)}, u32[]{:S(2)}) collective-permute-start(bf16[512,384]{1,0:T(8,128)(2,1)} %get-tuple-element.15), channel_id=1, source_target_pairs={{0,1},{1,2},{2,3},{3,4},{4,5},{5,6},{6,7},{7,8},{8,9},{9,10},{10,1... | collective-permute-start | bytes 1179656 | tf_op jit(solution)/shard_map/ppermute | solution.py:362
  30.1 1.3 %collective-permute-start.1 = (bf16[512,384]{1,0:T(8,128)(2,1)}, bf16[512,384]{1,0:T(8,128)(2,1)S(1)}, u32[]{:S(2)}, u32[]{:S(2)}) collective-permute-start(bf16[512,384]{1,0:T(8,128)(2,1)} %get-tuple-element.16), channel_id=1, source_target_pairs={{1,0},{2,1},{3,2},{4,3},{5,4},{6,5},{7,6},{8,7},{9,8},{10,9},{11,1... | collective-permute-start | bytes 1179656 | tf_op jit(solution)/shard_map/ppermute | solution.py:362
  31.4 4.9 %all-to-all-done.received = bf16[32,3,8,128]{3,2,1,0:T(8,128)(2,1)S(1)} async-done(((bf16[32,3,8,128]{3,2,1,0:T(8,128)(2,1)}), bf16[32,3,8,128]{3,2,1,0:T(8,128)(2,1)S(1)}, u32[]{:S(2)}, u32[]{:S(2)}) %all-to-all-start) | async-done | bytes 196640 | tf_op jit(solution)/shard_map/all_to_all | solution.py:356
  36.4 12.2 %all_to_all.15.roots = bf16[8,8,128]{2,1,0:T(8,128)(2,1)S(1)} all-to-all(bf16[8,8,128]{2,1,0:T(8,128)(2,1)S(1)} %shard_map.137), channel_id=1, replica_groups=mesh['leaf'=8,'sub'=32] {'leaf'}, dimensions={0} | all-to-all | bytes 32768 | tf_op jit(solution)/shard_map/all_to_all | solution.py:356
  48.6 0.0 copy-done
  48.6 1.5 %shard_map.138 = bf16[32,5,8,128]{3,2,1,0:T(8,128)(2,1)} custom-call(s32[1,2]{1,0:T(1,128)S(1)} %copy-done, bf16[32,3,8,128]{3,2,1,0:T(8,128)(2,1)S(1)} %all-to-all-done.received, bf16[8,8,128]{2,1,0:T(8,128)(2,1)S(1)} %all_to_all.15.roots), custom_call_target="tpu_custom_call" | custom-call | tf_op jit(solution)/shard_map/pallas_call | solution.py:366
  50.1 4.8 %all-to-all-start.2 = ((bf16[32,5,8,128]{3,2,1,0:T(8,128)(2,1)}), bf16[32,5,8,128]{3,2,1,0:T(8,128)(2,1)S(1)}, u32[]{:S(2)}, u32[]{:S(2)}) async-start(bf16[32,5,8,128]{3,2,1,0:T(8,128)(2,1)} %shard_map.138), calls=%async_computation.2 | async-start | bytes 655360 | tf_op jit(solution)/shard_map/all_to_all | solution.py:356
  55.6 0.0 copy-done.1
  55.6 6.3 %shard_map.139.rest_0_ = f32[3,512,256]{2,1,0:T(8,128)} custom-call(s32[2]{0:T(128)} %pad_add_fusion.position, s32[3,8]{1,0:T(4,128)S(1)} %bitcast.5, s32[8]{0:T(128)} %near_count.3, bf16[8,512,128]{2,1,0:T(8,128)(2,1)} %get-tuple-element.13.rows_hbm, bf16[8,512,384]{2,1,0:T(8,128)(2,1)} %get-tuple-element.14.cols_hbm), custom_call_target="tpu_custom_call" | custom-call | flops 3221225472 | bytes 6291456 | tf_op jit(solution)/shard_map/pallas_call | solution.py:366
  61.9 0.0 collective-permute-done.rest_0_
  61.9 0.0 collective-permute-done.1.rest_1_
  61.9 8.6 %shard_map.140.rest_1_ = f32[5,512,256]{2,1,0:T(8,128)} custom-call(s32[2]{0:T(128)} %pad_add_fusion.position, s32[3,8]{1,0:T(4,128)S(1)} %bitcast.6, s32[8]{0:T(128)} %near_count.3, bf16[8,512,128]{2,1,0:T(8,128)(2,1)} %get-tuple-element.13.rows_hbm, bf16[8,512,384]{2,1,0:T(8,128)(2,1)} %get-tuple-element.14.cols_hbm, ...), custom_call_target="tpu_custom_call" | custom-call | flops 3221225472 | bytes 6291456 | tf_op jit(solution)/shard_map/pallas_call | solution.py:366
  70.5 0.0 all-to-all-done.2.received
  70.5 13.3 %shard_map.141 = f32[4096,2,128]{2,1,0:T(2,128)} custom-call(s32[1,4096]{1,0:T(1,128)} %order.3, s32[1]{0:T(128)S(6)} %copy.15.pair_count, bf16[32,5,8,128]{3,2,1,0:T(8,128)(2,1)S(1)} %all-to-all-done.2.received, bf16[1,3,128,128]{3,2,1,0:T(8,128)(2,1)} %pair_hbm.1, bf16[1,2,128,128]{3,2,1,0:T(8,128)(2,1)} %top_hbm.1, ...), custom_call_target="tpu_custom_call" | custom-call | flops 536870912 | bytes 1048576 | tf_op jit(solution)/shard_map/pallas_call | solution.py:366
  (1 shorter events, 0.0 us)
Async XLA Ops:
  0.6 48.0 %copy-start = (s32[1,2]{1,0:T(1,128)S(1)}, s32[1,2]{1,0:T(1,128)}, u32[]{:S(2)}) copy-start(s32[1,2]{1,0:T(1,128)} %top_list.1) | copy-start | bytes 28
  0.6 55.0 %copy-start.1 = (s32[8,3]{0,1:T(4,128)S(1)}, s32[8,3]{0,1:T(4,128)}, u32[]{:S(2)}) copy-start(s32[8,3]{0,1:T(4,128)} %param.21) | copy-start | bytes 292
  15.1 21.3 %all-to-all-start = ((bf16[32,3,8,128]{3,2,1,0:T(8,128)(2,1)}), bf16[32,3,8,128]{3,2,1,0:T(8,128)(2,1)S(1)}, u32[]{:S(2)}, u32[]{:S(2)}) async-start(bf16[32,3,8,128]{3,2,1,0:T(8,128)(2,1)} %get-tuple-element.11), calls=%async_computation | async-start | bytes 393216 | tf_op jit(solution)/shard_map/all_to_all | solution.py:356
  26.9 35.0 %collective-permute-start = (bf16[512,384]{1,0:T(8,128)(2,1)}, bf16[512,384]{1,0:T(8,128)(2,1)S(1)}, u32[]{:S(2)}, u32[]{:S(2)}) collective-permute-start(bf16[512,384]{1,0:T(8,128)(2,1)} %get-tuple-element.15), channel_id=1, source_target_pairs={{0,1},{1,2},{2,3},{3,4},{4,5},{5,6},{6,7},{7,8},{8,9},{9,10},{10,1... | collective-permute-start | bytes 1179656 | tf_op jit(solution)/shard_map/ppermute | solution.py:362
  30.1 31.8 %collective-permute-start.1 = (bf16[512,384]{1,0:T(8,128)(2,1)}, bf16[512,384]{1,0:T(8,128)(2,1)S(1)}, u32[]{:S(2)}, u32[]{:S(2)}) collective-permute-start(bf16[512,384]{1,0:T(8,128)(2,1)} %get-tuple-element.16), channel_id=1, source_target_pairs={{1,0},{2,1},{3,2},{4,3},{5,4},{6,5},{7,6},{8,7},{9,8},{10,9},{11,1... | collective-permute-start | bytes 1179656 | tf_op jit(solution)/shard_map/ppermute | solution.py:362
  50.1 20.5 %all-to-all-start.2 = ((bf16[32,5,8,128]{3,2,1,0:T(8,128)(2,1)}), bf16[32,5,8,128]{3,2,1,0:T(8,128)(2,1)S(1)}, u32[]{:S(2)}, u32[]{:S(2)}) async-start(bf16[32,5,8,128]{3,2,1,0:T(8,128)(2,1)} %shard_map.138), calls=%async_computation.2 | async-start | bytes 655360 | tf_op jit(solution)/shard_map/all_to_all | solution.py:356

commit v3 on v2

--- a/solution.py
+++ b/solution.py
@@ -14,7 +14,6 @@
 SMALL_LIMIT = 4 << 20
 FINAL_LIMIT = 40 << 20
 NEAR_LIMIT = 40 << 20
-UNROLL = 64
 BLOCK = 512
 NEAR_GROUPS = ((1, 2, 3), (4, 5, 6, 0, 7))
 
@@ -46,15 +45,6 @@
 def high_low(x):
     high = x.astype(bf16)
     return high, (x - high.astype(f32)).astype(bf16)
-
-
-def row_loop(rows, step):
-    def several(i, carry):
-        for k in range(UNROLL):
-            step(i * UNROLL + k)
-        return carry
-
-    lax.fori_loop(0, rows // UNROLL, several, 0)
 
 
 def chunk_loop(rows, size, step):
@@ -93,6 +83,7 @@
     held_points,
     sems,
     out_sems,
+    edge_sems,
 ):
     leaves, leaf_rows, rank = basis.shape
     features, per_dev = points.shape
@@ -138,42 +129,53 @@
     copies[0].wait()
     chunk_loop(per_dev, BLOCK, augment)
 
-    def move(p):
-        source = order[0, p]
-        held_vals[p] = vectors[source]
-        held_points[pl.ds(p, 1), :] = table[pl.ds(source, 1), :]
-
-    copies[1].wait()
-    row_loop(per_dev, move)
-
-    for copy in copies[2:]:
+    def move_leaf(leaf):
+        start = pl.multiple_of(leaf * leaf_rows, leaf_rows)
+        for k in range(leaf_rows):
+            source = order[0, start + k]
+            held_vals[start + k] = vectors[source]
+            held_points[pl.ds(start + k, 1), :] = table[pl.ds(source, 1), :]
+
+    for copy in copies[1:]:
         copy.wait()
     ones_left = (piece >= 0) & (piece < 3)
     ones_right = (piece >= 3) & (piece < 6)
-    stores = []
-    node = jnp.zeros((rank, width), f32)
-    for leaf in range(leaves):
-        base = leaf * leaf_rows
-        vals = held_vals[base : base + leaf_rows].reshape(leaf_rows, width)
-        got = held_points[base : base + leaf_rows, :]
+
+    def stores_of(leaf):
+        return [
+            pltpu.make_async_copy(vals_cols.at[leaf], vals_cols_hbm.at[leaf], out_sems.at[leaf, 0]),
+            pltpu.make_async_copy(rows_aug.at[leaf], rows_aug_hbm.at[leaf], out_sems.at[leaf, 1]),
+        ]
+
+    def form(leaf):
+        start = pl.multiple_of(leaf * leaf_rows, leaf_rows)
+        vals = held_vals[pl.ds(start, leaf_rows)].reshape(leaf_rows, width)
+        got = held_points[pl.ds(start, leaf_rows), :]
         cols = jnp.where(ones_left, 1.0, got).astype(bf16)
         vals_cols[leaf, :, 0:width] = vals
         vals_cols[leaf, :, width : width + LANES] = cols
         rows_aug[leaf] = jnp.where(ones_right, 1.0, got).astype(bf16)
-        places = [
-            (vals_cols.at[leaf], vals_cols_hbm.at[leaf], 2 * leaf),
-            (rows_aug.at[leaf], rows_aug_hbm.at[leaf], 2 * leaf + 1),
-        ]
-        if leaf == 0:
-            places.append((vals_cols.at[leaf], first_hbm, 2 * leaves))
-        if leaf == leaves - 1:
-            places.append((vals_cols.at[leaf], last_hbm, 2 * leaves + 1))
-        for source, target, slot in places:
-            stores.append(pltpu.make_async_copy(source, target, out_sems.at[slot]))
-            stores[-1].start()
         coef = tn_dot(basis[leaf], vals)
         high, low = high_low(coef)
-        node = node + tn_dot(transfer[leaf], high) + tn_dot(transfer[leaf], low)
+        return tn_dot(transfer[leaf], high) + tn_dot(transfer[leaf], low)
+
+    def one_leaf(leaf, total):
+        total = total + form(leaf)
+        move_leaf(leaf + 1)
+        for copy in stores_of(leaf):
+            copy.start()
+        return total
+
+    move_leaf(0)
+    last = leaves - 1
+    node = lax.fori_loop(0, last, one_leaf, jnp.zeros((rank, width), f32))
+    node = node + form(last)
+    edges = [
+        pltpu.make_async_copy(vals_cols.at[0], first_hbm, edge_sems.at[0]),
+        pltpu.make_async_copy(vals_cols.at[last], last_hbm, edge_sems.at[1]),
+    ]
+    for copy in stores_of(last) + edges:
+        copy.start()
 
     product = mats[0].astype(f32)
     for depth in range(1, levels):
@@ -191,7 +193,10 @@
         send[c, 0] = node[r : r + SUBLANES, q : q + LANES].astype(bf16)
         send[c, 1] = lifted[r : r + SUBLANES, q : q + LANES].astype(bf16)
         send[c, 2] = request.astype(bf16)
-    for copy in stores:
+    for leaf in range(leaves):
+        for copy in stores_of(leaf):
+            copy.wait()
+    for copy in edges:
         copy.wait()
 
 
@@ -338,18 +343,28 @@
     small[2].wait()
     small[3].wait()
     for leaf in range(leaves):
+        large[leaf].wait()
+
+    def move_leaf(leaf):
+        start = pl.multiple_of(leaf * leaf_rows, leaf_rows)
+        for k in range(leaf_rows):
+            out[order[0, start + k]] = held[start + k]
+
+    def form(leaf):
         field = (nn_dot(transfer[leaf], high) + nn_dot(transfer[leaf], low)).astype(bf16)
-        far = nn_dot(basis[leaf], field)
-        large[leaf].wait()
-        total = far + near[leaf]
-        r = pl.ds(leaf * leaf_rows, leaf_rows)
+        total = nn_dot(basis[leaf], field) + near[leaf]
+        r = pl.ds(pl.multiple_of(leaf * leaf_rows, leaf_rows), leaf_rows)
         for q in range(across):
             held[r, q, :] = total[:, q * LANES : (q + 1) * LANES]
 
-    def move(p):
-        out[order[0, p]] = held[p]
-
-    row_loop(leaves * leaf_rows, move)
+    def one_leaf(leaf, carry):
+        move_leaf(leaf - 1)
+        form(leaf)
+        return carry
+
+    form(0)
+    lax.fori_loop(1, leaves, one_leaf, 0)
+    move_leaf(leaves - 1)
 
 
 def exchange(array, axis):
@@ -445,7 +460,8 @@
             pltpu.VMEM(vectors.shape, bf16),
             pltpu.VMEM((per_dev, LANES), f32),
             pltpu.SemaphoreType.DMA((4 + levels_count,)),
-            pltpu.SemaphoreType.DMA((2 * leaf_count + 2,)),
+            pltpu.SemaphoreType.DMA((leaf_count, 2)),
+            pltpu.SemaphoreType.DMA((2,)),
         ),
         (ANY_SPEC,) * 4 + (VMEM_SPEC,) * 2,
         flops=1 << 29,

time: 84.6 us -> 84.9 us (level)
  no operation moved by 1% of the time
where the time goes in v3:
time: 84.9 us; the launch traced here: 84.4 us
  Pallas kernels  44.4 us (52%)
  starting transfers between devices  21.3 us (25%)
  blocking collectives  12.2 us (14%)
  waiting for transfers between devices  4.93 us (6%)
  between operations  0.9 us (1%)
    pallas_call x6, Pallas kernels, call(): pl.pallas_call(kernel, out_shape=outs, in_specs=specs, out_specs=jax.tree...  44.4 us
    all_to_all x2, starting transfers between devices, exchange(): return lax.all_to_all(array, axis, 0, 0, tiled=True)  16.9 us
    all_to_all x1, blocking collectives, exchange(): return lax.all_to_all(array, axis, 0, 0, tiled=True)  12.2 us
    all_to_all x2, waiting for transfers between devices, exchange(): return lax.all_to_all(array, axis, 0, 0, tiled=True)  4.93 us
    ppermute x2, starting transfers between devices, shifted(): return lax.ppermute(block, axis, route)  4.45 us
  transfers between devices with their start and end apart: 4, of which 1 were waited for; matrix products, arithmetic and copies ran while one was open for 0% of the time, Pallas kernels for 20%

profile of v3, /device:TPU:1, one launch (start us, length us, event | category | flops | bytes accessed | tf_op | source)
XLA Modules:
  0.0 84.4 jit_solution(12880646944364738149)
XLA Ops:
  0.0 0.6 pad_add_fusion.position
  0.6 0.0 copy-start
  0.6 0.0 copy-start.1
  0.6 14.3 %shard_map.136 = (bf16[8,512,384]{2,1,0:T(8,128)(2,1)}, bf16[8,512,128]{2,1,0:T(8,128)(2,1)}, bf16[512,384]{1,0:T(8,128)(2,1)}, bf16[512,384]{1,0:T(8,128)(2,1)}...) custom-call(s32[1,4096]{1,0:T(1,128)} %order.3, s32[2]{0:T(128)} %pad_add_fusion.position, s32[1,3]{1,0:T(1,128)} %pair_list.1, ...), custom_call_target="tpu_custom_call" | custom-call | flops 536870912 | bytes 1048576 | tf_op jit(solution)/shard_map/pallas_call | solution.py:381
  14.9 11.9 %all-to-all-start = ((bf16[32,3,8,128]{3,2,1,0:T(8,128)(2,1)}), bf16[32,3,8,128]{3,2,1,0:T(8,128)(2,1)S(1)}, u32[]{:S(2)}, u32[]{:S(2)}) async-start(bf16[32,3,8,128]{3,2,1,0:T(8,128)(2,1)} %get-tuple-element.11), calls=%async_computation | async-start | bytes 393216 | tf_op jit(solution)/shard_map/all_to_all | solution.py:371
  26.8 3.2 %collective-permute-start = (bf16[512,384]{1,0:T(8,128)(2,1)}, bf16[512,384]{1,0:T(8,128)(2,1)S(1)}, u32[]{:S(2)}, u32[]{:S(2)}) collective-permute-start(bf16[512,384]{1,0:T(8,128)(2,1)} %get-tuple-element.15), channel_id=1, source_target_pairs={{0,1},{1,2},{2,3},{3,4},{4,5},{5,6},{6,7},{7,8},{8,9},{9,10},{10,1... | collective-permute-start | bytes 1179656 | tf_op jit(solution)/shard_map/ppermute | solution.py:377
  29.9 1.3 %collective-permute-start.1 = (bf16[512,384]{1,0:T(8,128)(2,1)}, bf16[512,384]{1,0:T(8,128)(2,1)S(1)}, u32[]{:S(2)}, u32[]{:S(2)}) collective-permute-start(bf16[512,384]{1,0:T(8,128)(2,1)} %get-tuple-element.16), channel_id=1, source_target_pairs={{1,0},{2,1},{3,2},{4,3},{5,4},{6,5},{7,6},{8,7},{9,8},{10,9},{11,1... | collective-permute-start | bytes 1179656 | tf_op jit(solution)/shard_map/ppermute | solution.py:377
  31.2 4.9 %all-to-all-done.received = bf16[32,3,8,128]{3,2,1,0:T(8,128)(2,1)S(1)} async-done(((bf16[32,3,8,128]{3,2,1,0:T(8,128)(2,1)}), bf16[32,3,8,128]{3,2,1,0:T(8,128)(2,1)S(1)}, u32[]{:S(2)}, u32[]{:S(2)}) %all-to-all-start) | async-done | bytes 196640 | tf_op jit(solution)/shard_map/all_to_all | solution.py:371
  36.2 12.2 %all_to_all.15.roots = bf16[8,8,128]{2,1,0:T(8,128)(2,1)S(1)} all-to-all(bf16[8,8,128]{2,1,0:T(8,128)(2,1)S(1)} %shard_map.137), channel_id=1, replica_groups=mesh['leaf'=8,'sub'=32] {'leaf'}, dimensions={0} | all-to-all | bytes 32768 | tf_op jit(solution)/shard_map/all_to_all | solution.py:371
  48.4 0.0 copy-done
  48.4 1.5 %shard_map.138 = bf16[32,5,8,128]{3,2,1,0:T(8,128)(2,1)} custom-call(s32[1,2]{1,0:T(1,128)S(1)} %copy-done, bf16[32,3,8,128]{3,2,1,0:T(8,128)(2,1)S(1)} %all-to-all-done.received, bf16[8,8,128]{2,1,0:T(8,128)(2,1)S(1)} %all_to_all.15.roots), custom_call_target="tpu_custom_call" | custom-call | tf_op jit(solution)/shard_map/pallas_call | solution.py:381
  49.9 5.0 %all-to-all-start.2 = ((bf16[32,5,8,128]{3,2,1,0:T(8,128)(2,1)}), bf16[32,5,8,128]{3,2,1,0:T(8,128)(2,1)S(1)}, u32[]{:S(2)}, u32[]{:S(2)}) async-start(bf16[32,5,8,128]{3,2,1,0:T(8,128)(2,1)} %shard_map.138), calls=%async_computation.2 | async-start | bytes 655360 | tf_op jit(solution)/shard_map/all_to_all | solution.py:371
  55.6 0.0 copy-done.1
  55.6 6.3 %shard_map.139.rest_0_ = f32[3,512,256]{2,1,0:T(8,128)} custom-call(s32[2]{0:T(128)} %pad_add_fusion.position, s32[3,8]{1,0:T(4,128)S(1)} %bitcast.5, s32[8]{0:T(128)} %near_count.3, bf16[8,512,128]{2,1,0:T(8,128)(2,1)} %get-tuple-element.13.rows_hbm, bf16[8,512,384]{2,1,0:T(8,128)(2,1)} %get-tuple-element.14.cols_hbm), custom_call_target="tpu_custom_call" | custom-call | flops 3221225472 | bytes 6291456 | tf_op jit(solution)/shard_map/pallas_call | solution.py:381
  61.9 0.0 collective-permute-done.rest_0_
  61.9 0.0 collective-permute-done.1.rest_1_
  62.0 8.6 %shard_map.140.rest_1_ = f32[5,512,256]{2,1,0:T(8,128)} custom-call(s32[2]{0:T(128)} %pad_add_fusion.position, s32[3,8]{1,0:T(4,128)S(1)} %bitcast.6, s32[8]{0:T(128)} %near_count.3, bf16[8,512,128]{2,1,0:T(8,128)(2,1)} %get-tuple-element.13.rows_hbm, bf16[8,512,384]{2,1,0:T(8,128)(2,1)} %get-tuple-element.14.cols_hbm, ...), custom_call_target="tpu_custom_call" | custom-call | flops 3221225472 | bytes 6291456 | tf_op jit(solution)/shard_map/pallas_call | solution.py:381
  70.6 0.0 all-to-all-done.2.received
  70.6 13.7 %shard_map.141 = f32[4096,2,128]{2,1,0:T(2,128)} custom-call(s32[1,4096]{1,0:T(1,128)} %order.3, s32[1]{0:T(128)S(6)} %copy.15.pair_count, bf16[32,5,8,128]{3,2,1,0:T(8,128)(2,1)S(1)} %all-to-all-done.2.received, bf16[1,3,128,128]{3,2,1,0:T(8,128)(2,1)} %pair_hbm.1, bf16[1,2,128,128]{3,2,1,0:T(8,128)(2,1)} %top_hbm.1, ...), custom_call_target="tpu_custom_call" | custom-call | flops 536870912 | bytes 1048576 | tf_op jit(solution)/shard_map/pallas_call | solution.py:381
  (1 shorter events, 0.0 us)
Async XLA Ops:
  0.6 47.8 %copy-start = (s32[1,2]{1,0:T(1,128)S(1)}, s32[1,2]{1,0:T(1,128)}, u32[]{:S(2)}) copy-start(s32[1,2]{1,0:T(1,128)} %top_list.1) | copy-start | bytes 28
  0.6 55.0 %copy-start.1 = (s32[8,3]{0,1:T(4,128)S(1)}, s32[8,3]{0,1:T(4,128)}, u32[]{:S(2)}) copy-start(s32[8,3]{0,1:T(4,128)} %param.21) | copy-start | bytes 292
  14.9 21.3 %all-to-all-start = ((bf16[32,3,8,128]{3,2,1,0:T(8,128)(2,1)}), bf16[32,3,8,128]{3,2,1,0:T(8,128)(2,1)S(1)}, u32[]{:S(2)}, u32[]{:S(2)}) async-start(bf16[32,3,8,128]{3,2,1,0:T(8,128)(2,1)} %get-tuple-element.11), calls=%async_computation | async-start | bytes 393216 | tf_op jit(solution)/shard_map/all_to_all | solution.py:371
  26.8 35.2 %collective-permute-start = (bf16[512,384]{1,0:T(8,128)(2,1)}, bf16[512,384]{1,0:T(8,128)(2,1)S(1)}, u32[]{:S(2)}, u32[]{:S(2)}) collective-permute-start(bf16[512,384]{1,0:T(8,128)(2,1)} %get-tuple-element.15), channel_id=1, source_target_pairs={{0,1},{1,2},{2,3},{3,4},{4,5},{5,6},{6,7},{7,8},{8,9},{9,10},{10,1... | collective-permute-start | bytes 1179656 | tf_op jit(solution)/shard_map/ppermute | solution.py:377
  29.9 32.0 %collective-permute-start.1 = (bf16[512,384]{1,0:T(8,128)(2,1)}, bf16[512,384]{1,0:T(8,128)(2,1)S(1)}, u32[]{:S(2)}, u32[]{:S(2)}) collective-permute-start(bf16[512,384]{1,0:T(8,128)(2,1)} %get-tuple-element.16), channel_id=1, source_target_pairs={{1,0},{2,1},{3,2},{4,3},{5,4},{6,5},{7,6},{8,7},{9,8},{10,9},{11,1... | collective-permute-start | bytes 1179656 | tf_op jit(solution)/shard_map/ppermute | solution.py:377
  49.9 20.6 %all-to-all-start.2 = ((bf16[32,5,8,128]{3,2,1,0:T(8,128)(2,1)}), bf16[32,5,8,128]{3,2,1,0:T(8,128)(2,1)S(1)}, u32[]{:S(2)}, u32[]{:S(2)}) async-start(bf16[32,5,8,128]{3,2,1,0:T(8,128)(2,1)} %shard_map.138), calls=%async_computation.2 | async-start | bytes 655360 | tf_op jit(solution)/shard_map/all_to_all | solution.py:371
